TPU v7x, 128 devices: a whole 4x4x4 slice. The times are simulated.
128 devices in a mesh: section: 16 (over x_hi, y, core), expert: 8 (over z, x_lo).
Axes of the slice: x: 4 (x_hi: 2, x_lo: 2; x = x_hi * 2 + x_lo), y: 4, z: 4, core: 2. Of those that a mesh axis runs over, the one named last changes fastest.
Arguments:
- fwd_input: bfloat16 [16, 1024, 2560], P('section', 'expert'), may hold values from -6 to 6
- back_input: bfloat16 [16, 1024, 2560], P('section', 'expert'), may hold values from -6 to 6
- cot_input: bfloat16 [16, 1024, 2560], P('section', 'expert'), may hold values from -6 to 6
- fwd_routes: int32 [16, 1024, 2], P('section', 'expert'), may hold values from 0 to 7, all different within a row; in each aligned block of 128 rows (0 to 127, 128 to 255, ..., all dimensions but the last counted through in order) at most 64 rows name the same one
- back_routes: int32 [16, 1024, 2], P('section', 'expert'), may hold values from 0 to 7, all different within a row; in each aligned block of 128 rows (0 to 127, 128 to 255, ..., all dimensions but the last counted through in order) at most 64 rows name the same one
- fwd_gates: float32 [16, 1024, 2], P('section', 'expert'), may hold values from 0.05 to 1
- back_gates: float32 [16, 1024, 2], P('section', 'expert'), may hold values from 0.05 to 1
- w_gate: bfloat16 [16, 8, 2560, 768], P('section', 'expert'), may hold values from -0.125 to 0.125
- w_up: bfloat16 [16, 8, 2560, 768], P('section', 'expert'), may hold values from -0.125 to 0.125
- w_down: bfloat16 [16, 8, 768, 2560], P('section', 'expert'), may hold values from -0.21875 to 0.21875
- norm_gain: float32 [16, 2560], P('section'), may hold values from 0.1 to 1.9
- verdict_head: float32 [2560], replicated, may hold values from -0.125 to 0.125
- verdict_labels: int32 [1024], P('expert'), may hold values from 0 to 1
Outputs:
- next_input: bfloat16 [16, 1024, 2560], P('section', 'expert')
- prev_grad: bfloat16 [16, 1024, 2560], P('section', 'expert')
- gain_grad: float32 [16, 2560], P('section')
- grad_gate: bfloat16 [16, 8, 2560, 768], P('section', 'expert')
- grad_up: bfloat16 [16, 8, 2560, 768], P('section', 'expert')
- grad_down: bfloat16 [16, 8, 768, 2560], P('section', 'expert')
Inputs may be any that keep to these rules, and one draw needn't show every extreme that they name: `fwd_routes`: each row names 2 different experts; within the rows of one device no expert is named by more than 64 rows, a bound that some block reaches. `back_routes`: as for fwd_routes.
All inputs are finite; a program needn't handle non-finite values.
Results may differ from a plain program's by a relative error of at most 0.012.
Values may be sent and summed in bfloat16 or wider, within the bound.
No kernel may reach another device: no remote copies, remote signals or barrier semaphores. Data moves between devices by JAX's collectives and lax.ppermute only.
A program may use at most 128 MiB of HBM per device.

v0:
```python
import jax
import jax.numpy as jnp
from jax import lax
from jax.experimental import pallas as pl
from jax.experimental.pallas import tpu as pltpu
from jax.sharding import PartitionSpec as P

loss_scale = 64.0
norm_eps = 1e-06
bf16 = jnp.bfloat16
f32 = jnp.float32
chunk = 512
vmem = pl.BlockSpec(memory_space=pltpu.VMEM)
smem = pl.BlockSpec(memory_space=pltpu.SMEM)


def passed_along(value, axis, steps):
    count = lax.axis_size(axis)
    initial, last = (max(0, -steps), min(count, count - steps))
    return lax.ppermute(value, axis, [(source, source + steps) for source in range(initial, last)])


def slot_keys(ids, groups, capacity):
    tokens = ids.shape[0]
    lanes = lax.broadcasted_iota(jnp.int32, (tokens, 128), 1)
    hit0 = ids[:, 0:1] == lanes
    hit1 = ids[:, 1:2] == lanes
    hits = (hit0 | hit1).astype(bf16)
    before = (
        lax.broadcasted_iota(jnp.int32, (tokens, tokens), 1)
        < lax.broadcasted_iota(jnp.int32, (tokens, tokens), 0)
    ).astype(bf16)
    ranks = jnp.dot(before, hits, preferred_element_type=f32)
    rank0 = jnp.sum(jnp.where(hit0, ranks, 0.0), axis=1, keepdims=True).astype(jnp.int32)
    rank1 = jnp.sum(jnp.where(hit1, ranks, 0.0), axis=1, keepdims=True).astype(jnp.int32)
    return ids[:, 0:1] * capacity + rank0, ids[:, 1:2] * capacity + rank1


def slot_hits(ids, groups, capacity):
    key0, key1 = slot_keys(ids, groups, capacity)
    slots = lax.broadcasted_iota(jnp.int32, (ids.shape[0], groups * capacity), 1)
    return key0 == slots, key1 == slots


def split_weights(hit0, hit1, gates):
    weights = jnp.where(hit0, gates[:, 0:1], 0.0) + jnp.where(hit1, gates[:, 1:2], 0.0)
    high = weights.astype(bf16)
    low = (weights - high.astype(f32)).astype(bf16)
    return high, low


def over_tokens(left, right):
    return lax.dot_general(left, right, (((0,), (0,)), ((), ())), preferred_element_type=f32)


def inv_rms_of(rows):
    return lax.rsqrt(jnp.mean(rows * rows, axis=-1, keepdims=True) + norm_eps)


def chunks(width):
    return [slice(at, min(at + chunk, width)) for at in range(0, width, chunk)]


def send_forward(groups, capacity, x_ref, gain_ref, ids_ref, out_ref):
    hit0, hit1 = slot_hits(ids_ref[...], groups, capacity)
    pick = (hit0 | hit1).astype(bf16)
    x = x_ref[...].astype(f32)
    normed = (x * inv_rms_of(x) * gain_ref[...]).astype(bf16)
    for cols in chunks(x.shape[1]):
        out_ref[:, cols] = over_tokens(pick, normed[:, cols]).astype(bf16)


def send_backward(
    groups,
    capacity,
    last_ref,
    fwd_ref,
    back_ref,
    cot_ref,
    gain_ref,
    head_ref,
    fwd_ids_ref,
    back_ids_ref,
    fwd_gates_ref,
    back_gates_ref,
    rows_ref,
    dout_ref,
):
    is_last = last_ref[0] == 1
    ids = jnp.where(is_last, fwd_ids_ref[...], back_ids_ref[...])
    gates = jnp.where(is_last, fwd_gates_ref[...], back_gates_ref[...])
    hit0, hit1 = slot_hits(ids, groups, capacity)
    pick = (hit0 | hit1).astype(bf16)
    high, low = split_weights(hit0, hit1, gates)
    x = jnp.where(is_last, fwd_ref[...].astype(f32), back_ref[...].astype(f32))
    normed = (x * inv_rms_of(x) * gain_ref[...]).astype(bf16)
    for cols in chunks(x.shape[1]):
        rows_ref[:, cols] = over_tokens(pick, normed[:, cols]).astype(bf16)
        cot = cot_ref[:, cols]
        head = jnp.broadcast_to(head_ref[:, cols], cot.shape)
        head_high = head.astype(bf16)
        head_low = (head - head_high.astype(f32)).astype(bf16)
        cot_high = jnp.where(is_last, head_high.astype(f32), cot.astype(f32)).astype(bf16)
        cot_low = jnp.where(is_last, head_low.astype(f32), 0.0).astype(bf16)
        dout_ref[:, cols] = (
            over_tokens(high, cot_high) + over_tokens(low, cot_high) + over_tokens(high, cot_low)
        ).astype(bf16)


def join_forward(
    groups,
    capacity,
    last_ref,
    ret_ref,
    x_ref,
    ids_ref,
    gates_ref,
    head_ref,
    labels_ref,
    out_ref,
    coef_ref,
    slots_ref,
):
    is_last = last_ref[0] == 1
    hit0, hit1 = slot_hits(ids_ref[...], groups, capacity)
    high, low = split_weights(hit0, hit1, gates_ref[...])
    logits = jnp.zeros((x_ref.shape[0], 1), f32)
    for cols in chunks(x_ref.shape[1]):
        ret = ret_ref[:, cols]
        mixed = jnp.dot(high, ret, preferred_element_type=f32) + jnp.dot(
            low, ret, preferred_element_type=f32
        )
        out = (x_ref[:, cols].astype(f32) + mixed).astype(bf16)
        out_ref[:, cols] = out
        logits += jnp.sum(out.astype(f32) * head_ref[:, cols], axis=1, keepdims=True)
    coef = loss_scale * (jax.nn.sigmoid(logits) - labels_ref[...].astype(f32))
    coef = jnp.where(is_last, coef, 1.0)
    coef_ref[...] = coef
    picked = jnp.sum(jnp.where(hit0 | hit1, coef, 0.0), axis=0, keepdims=True)
    slots_ref[...] = jnp.where(is_last, picked, 1.0)


def join_backward(
    groups,
    capacity,
    last_ref,
    ret_ref,
    fwd_ref,
    back_ref,
    cot_ref,
    coef_ref,
    gain_ref,
    head_ref,
    fwd_ids_ref,
    back_ids_ref,
    out_ref,
    grad_ref,
    normed_ref,
):
    is_last = last_ref[0] == 1
    ids = jnp.where(is_last, fwd_ids_ref[...], back_ids_ref[...])
    hit0, hit1 = slot_hits(ids, groups, capacity)
    pick = (hit0 | hit1).astype(bf16)
    coef = coef_ref[...]
    x = jnp.where(is_last, fwd_ref[...].astype(f32), back_ref[...].astype(f32))
    inv = inv_rms_of(x)
    dots = jnp.zeros((x.shape[0], 1), f32)
    for cols in chunks(x.shape[1]):
        d_normed = coef * jnp.dot(pick, ret_ref[:, cols], preferred_element_type=f32)
        normed_ref[:, cols] = d_normed
        product = d_normed * x[:, cols]
        dots += jnp.sum(product * gain_ref[:, cols], axis=1, keepdims=True)
        grad_ref[:, cols] = jnp.sum(product * inv, axis=0, keepdims=True)
    scale = inv * inv * inv * (dots / x.shape[1])
    for cols in chunks(x.shape[1]):
        cot = jnp.where(is_last, coef * head_ref[:, cols], cot_ref[:, cols].astype(f32))
        out_ref[:, cols] = (
            cot + inv * (gain_ref[:, cols] * normed_ref[:, cols]) - x[:, cols] * scale
        ).astype(bf16)


def call(kernel, name, outs, args, specs, scratch=()):
    return pl.pallas_call(
        kernel,
        out_shape=[jax.ShapeDtypeStruct(shape, dtype) for shape, dtype in outs],
        in_specs=specs,
        out_specs=[vmem] * len(outs),
        scratch_shapes=list(scratch),
        compiler_params=pltpu.CompilerParams(vmem_limit_bytes=48 << 20),
        name=name,
    )(*args)


def contract_rows(left_op, right_op):
    return lax.dot_general(
        left_op, right_op, (((0,), (0,)), ((), ())), preferred_element_type=f32
    )


def contract_cols(left_op, right_op):
    return lax.dot_general(
        left_op, right_op, (((1,), (1,)), ((), ())), preferred_element_type=f32
    )


def on_device(
    fwd_input,
    back_input,
    cot_input,
    fwd_routes,
    back_routes,
    fwd_gates,
    back_gates,
    w_gate,
    w_up,
    w_down,
    norm_gain,
    verdict_head,
    verdict_labels,
):
    sections = lax.axis_size("section")
    groups = lax.axis_size("expert")
    tok_dev, width = fwd_input.shape[1:]
    top_k = fwd_routes.shape[2]
    capacity = min(tok_dev, 2 * tok_dev * top_k // groups)
    slots = groups * capacity
    x_fwd, x_back, cot = fwd_input[0], back_input[0], cot_input[0]
    wg, wu, wd = w_gate[0, 0], w_up[0, 0], w_down[0, 0]
    head = verdict_head[None]
    last = (lax.axis_index("section") == sections - 1).astype(jnp.int32)[None]

    def bind(kernel):
        def bound(*refs):
            kernel(groups, capacity, *refs)

        return bound

    def exchange(value):
        out = lax.all_to_all(
            value.reshape(groups, capacity, width), "expert", split_axis=0, concat_axis=0, tiled=True
        )
        return out.reshape(slots, width)

    (send_f,) = call(
        bind(send_forward),
        "send_forward",
        [((slots, width), bf16)],
        (x_fwd, norm_gain, fwd_routes[0]),
        [vmem] * 3,
    )
    rows_f = exchange(send_f)
    send_b, send_d = call(
        bind(send_backward),
        "send_backward",
        [((slots, width), bf16)] * 2,
        (
            last,
            x_fwd,
            x_back,
            cot,
            norm_gain,
            head,
            fwd_routes[0],
            back_routes[0],
            fwd_gates[0],
            back_gates[0],
        ),
        [smem] + [vmem] * 9,
    )
    rows_f, send_b, send_d = lax.optimization_barrier((rows_f, send_b, send_d))
    rows_b = exchange(send_b)
    gate_pre = jnp.dot(rows_f, wg, preferred_element_type=f32)
    up_pre = jnp.dot(rows_f, wu, preferred_element_type=f32)
    hidden_f = (jax.nn.silu(gate_pre) * up_pre).astype(bf16)
    out_f = jnp.dot(hidden_f, wd, preferred_element_type=f32).astype(bf16)
    rows_b, send_d = lax.optimization_barrier((rows_b, send_d))
    rows_d = exchange(send_d)
    rows_d, out_f = lax.optimization_barrier((rows_d, out_f))
    ret_f = exchange(out_f)

    gate_pre = jnp.dot(rows_b, wg, preferred_element_type=f32)
    up_pre = jnp.dot(rows_b, wu, preferred_element_type=f32)
    sig = jax.nn.sigmoid(gate_pre)
    silu = gate_pre * sig
    hidden_b = (silu * up_pre).astype(bf16)
    d_hidden = contract_cols(rows_d, wd)
    d_gate = (d_hidden * up_pre * sig * (1.0 + gate_pre * (1.0 - sig))).astype(bf16)
    d_up = (d_hidden * silu).astype(bf16)
    d_rows = (contract_cols(d_gate, wg) + contract_cols(d_up, wu)).astype(bf16)

    ret_f, d_rows = lax.optimization_barrier((ret_f, d_rows))
    ret_d = exchange(d_rows)
    layer_out, coef, coef_slots = call(
        bind(join_forward),
        "join_forward",
        [((tok_dev, width), bf16), ((tok_dev, 1), f32), ((1, slots), f32)],
        (last, ret_f, x_fwd, fwd_routes[0], fwd_gates[0], head, verdict_labels[:, None]),
        [smem] + [vmem] * 6,
    )
    next_input = passed_along(layer_out, "section", 1)
    coef_rows = lax.all_to_all(
        coef_slots.reshape(groups, 1, capacity), "expert", split_axis=0, concat_axis=0, tiled=True
    ).reshape(slots, 1)

    def scaled(value):
        return (value.astype(f32) * coef_rows).astype(bf16)

    grad_d = contract_rows(scaled(hidden_b), rows_d).astype(bf16)
    grad_g = contract_rows(rows_b, scaled(d_gate)).astype(bf16)
    grad_u = contract_rows(rows_b, scaled(d_up)).astype(bf16)

    d_input, gain_local = call(
        bind(join_backward),
        "join_backward",
        [((tok_dev, width), bf16), ((1, width), f32)],
        (last, ret_d, x_fwd, x_back, cot, coef, norm_gain, head, fwd_routes[0], back_routes[0]),
        [smem] + [vmem] * 9,
        [pltpu.VMEM((tok_dev, width), f32)],
    )
    prev_grad = passed_along(d_input, "section", -1)
    shares = lax.all_to_all(
        jnp.broadcast_to(gain_local[None], (groups, 1, width)),
        "expert",
        split_axis=0,
        concat_axis=0,
        tiled=True,
    )
    gain_grad = jnp.sum(shares, axis=0)
    return (
        next_input[None],
        prev_grad[None],
        gain_grad,
        grad_g[None, None],
        grad_u[None, None],
        grad_d[None, None],
    )


def solution(mesh):
    return jax.shard_map(
        on_device,
        mesh=mesh,
        in_specs=(
            P("section", "expert", None),
            P("section", "expert", None),
            P("section", "expert", None),
            P("section", "expert", None),
            P("section", "expert", None),
            P("section", "expert", None),
            P("section", "expert", None),
            P("section", "expert", None, None),
            P("section", "expert", None, None),
            P("section", "expert", None, None),
            P("section", None),
            P(),
            P("expert"),
        ),
        out_specs=(
            P("section", "expert", None),
            P("section", "expert", None),
            P("section", None),
            P("section", "expert", None, None),
            P("section", "expert", None, None),
            P("section", "expert", None, None),
        ),
        check_vma=False,
    )
```

profile of v0, /device:TPU:4, one launch (start us, length us, event | category | flops | bytes accessed | tf_op | source)
XLA Modules:
  0.0 227.6 jit_solution(6740180986219971748)
XLA Ops:
  0.6 0.8 copy.36
  1.4 1.1 copy-done
  2.5 0.7 copy-done.6
  3.2 2.8 %send_forward.1 = bf16[512,2560]{1,0:T(8,128)(2,1)} custom-call(bf16[128,2560]{1,0:T(8,128)(2,1)S(1)} %bitcast.65, f32[1,2560]{1,0:T(1,128)S(1)} %copy-done.6, s32[128,2]{1,0:T(8,128)S(1)} %bitcast.73), custom_call_target="tpu_custom_call" | custom-call | tf_op jit(solution)/shard_map/send_forward/pallas_call | solution.py:183
  6.0 0.0 copy-start.1
  6.0 0.0 copy-start.2
  6.0 0.0 copy-start.4
  6.1 0.0 copy-start.7
  6.1 6.1 %all-to-all-start = ((bf16[8,64,2560]{2,1,0:T(8,128)(2,1)}), bf16[8,64,2560]{2,1,0:T(8,128)(2,1)}, u32[]{:S(2)}, u32[]{:S(2)}) async-start(bf16[8,64,2560]{2,1,0:T(8,128)(2,1)} %bitcast.3), calls=%async_computation | async-start | bytes 5242880 | tf_op jit(solution)/shard_map/all_to_all | solution.py:239
  12.2 0.0 copy-done.15
  12.2 0.1 copy.37
  12.3 0.1 copy.38
  12.4 0.1 copy.39
  12.6 5.4 %send_backward.1 = (bf16[512,2560]{1,0:T(8,128)(2,1)}, bf16[512,2560]{1,0:T(8,128)(2,1)}) custom-call(s32[1]{0:T(128)} %bitcast.refs_0_, bf16[128,2560]{1,0:T(8,128)(2,1)S(1)} %bitcast.66, bf16[128,2560]{1,0:T(8,128)(2,1)S(1)} %bitcast.69, bf16[128,2560]{1,0:T(8,128)(2,1)S(1)} %bitcast.71, f32[1,2560]{1,0:T(1,128)S(1)} %copy-done.7, ...), custom_call_target="tpu_custom_call" | custom-call | tf_op jit(solution)/shard_map/send_backward/pallas_call | solution.py:183
  18.0 26.9 %all-to-all-done = bf16[8,64,2560]{2,1,0:T(8,128)(2,1)} async-done(((bf16[8,64,2560]{2,1,0:T(8,128)(2,1)}), bf16[8,64,2560]{2,1,0:T(8,128)(2,1)}, u32[]{:S(2)}, u32[]{:S(2)}) %all-to-all-start) | async-done | bytes 2621472 | tf_op jit(solution)/shard_map/all_to_all | solution.py:239
  44.9 3.8 %all-to-all-start.1 = ((bf16[8,64,2560]{2,1,0:T(8,128)(2,1)}), bf16[8,64,2560]{2,1,0:T(8,128)(2,1)S(1)}, u32[]{:S(2)}, u32[]{:S(2)}) async-start(bf16[8,64,2560]{2,1,0:T(8,128)(2,1)} %bitcast.10), calls=%async_computation.1 | async-start | bytes 5242880 | tf_op jit(solution)/shard_map/all_to_all | solution.py:239
  48.6 0.1 copy.40.refs_6_
  48.8 31.7 %all-to-all-done.1 = bf16[8,64,2560]{2,1,0:T(8,128)(2,1)S(1)} async-done(((bf16[8,64,2560]{2,1,0:T(8,128)(2,1)}), bf16[8,64,2560]{2,1,0:T(8,128)(2,1)S(1)}, u32[]{:S(2)}, u32[]{:S(2)}) %all-to-all-start.1) | async-done | bytes 2621472 | tf_op jit(solution)/shard_map/all_to_all | solution.py:239
  80.5 4.4 %all-to-all-start.2 = ((bf16[8,64,2560]{2,1,0:T(8,128)(2,1)}), bf16[8,64,2560]{2,1,0:T(8,128)(2,1)}, u32[]{:S(2)}, u32[]{:S(2)}) async-start(bf16[8,64,2560]{2,1,0:T(8,128)(2,1)} %bitcast.87), calls=%async_computation.2 | async-start | bytes 5242880 | tf_op jit(solution)/shard_map/all_to_all | solution.py:239
  84.9 6.3 %fusion.15 = f32[512,768]{1,0:T(8,128)} fusion(bf16[512,2560]{1,0:T(8,128)(2,1)} %bitcast.4, bf16[1,1,2560,768]{3,2,1,0:T(8,128)(2,1)} %param.20), kind=kOutput, calls=%fused_computation.20 | convolution fusion | flops 2013265920 | bytes 8126464 | tf_op jit(solution)/shard_map/dot_general | solution.py:272
  91.2 11.6 %convolution_convert_fusion.3 = bf16[512,2560]{1,0:T(8,128)(2,1)} fusion(bf16[1,1,768,2560]{3,2,1,0:T(8,128)(2,1)} %param.22, f32[512,768]{1,0:T(8,128)} %fusion.15, bf16[512,2560]{1,0:T(8,128)(2,1)} %bitcast.4, bf16[1,1,2560,768]{3,2,1,0:T(8,128)(2,1)} %param.21), kind=kOutput, calls=%fused_computation.7 | convolution fusion | flops 4030201856 | bytes 14680064 | tf_op jit(solution)/shard_map/dot_general | solution.py:275
  102.7 5.5 %fusion.13 = f32[512,768]{1,0:T(8,128)} fusion(bf16[512,2560]{1,0:T(8,128)(2,1)S(1)} %bitcast.82, bf16[1,1,2560,768]{3,2,1,0:T(8,128)(2,1)} %param.20), kind=kOutput, calls=%fused_computation.18 | convolution fusion | flops 2013265920 | bytes 8126464 | tf_op jit(solution)/shard_map/dot_general | solution.py:281
  108.2 7.8 %all-to-all-done.2 = bf16[8,64,2560]{2,1,0:T(8,128)(2,1)} async-done(((bf16[8,64,2560]{2,1,0:T(8,128)(2,1)}), bf16[8,64,2560]{2,1,0:T(8,128)(2,1)}, u32[]{:S(2)}, u32[]{:S(2)}) %all-to-all-start.2) | async-done | bytes 2621472 | tf_op jit(solution)/shard_map/all_to_all | solution.py:239
  116.0 3.8 %all-to-all-start.3 = ((bf16[8,64,2560]{2,1,0:T(8,128)(2,1)}), bf16[8,64,2560]{2,1,0:T(8,128)(2,1)S(1)}, u32[]{:S(2)}, u32[]{:S(2)}) async-start(bf16[8,64,2560]{2,1,0:T(8,128)(2,1)} %bitcast.88), calls=%async_computation.3 | async-start | bytes 5242880 | tf_op jit(solution)/shard_map/all_to_all | solution.py:239
  119.9 0.0 copy-start.20
  119.9 0.0 copy-start.25
  119.9 5.2 %fusion.7 = f32[512,768]{1,0:T(8,128)S(1)} fusion(bf16[512,2560]{1,0:T(8,128)(2,1)} %bitcast.83, bf16[1,1,2560,768]{3,2,1,0:T(8,128)(2,1)} %param.21), kind=kOutput, calls=%fused_computation.12 | convolution fusion | flops 2013265920 | bytes 8126464 | tf_op jit(solution)/shard_map/dot_general | solution.py:282
  125.2 0.0 copy-start.21
  125.2 4.9 %multiply_convert_fusion.4 = (bf16[512,768]{1,0:T(8,128)(2,1)S(1)}, bf16[512,768]{1,0:T(8,128)(2,1)S(1)}) fusion(f32[512,768]{1,0:T(8,128)S(1)} %copy-done.25, f32[512,768]{1,0:T(8,128)S(1)} %fusion.7, bf16[512,2560]{1,0:T(8,128)(2,1)} %bitcast.13, bf16[1,1,768,2560]{3,2,1,0:T(8,128)(2,1)S(1)} %copy-done.20), kind=kOutput, calls=%fused_computation.26 | convolution fusion | flops 2018377728 | bytes 11272192 | tf_op jit(solution)/shard_map/dot_general | solution.py:201
  130.1 0.0 copy-done.26
  130.1 0.0 copy-start.22
  130.1 2.2 fusion.11
  132.4 0.4 copy-done.22
  132.8 3.7 %add_convert_fusion = bf16[512,2560]{1,0:T(8,128)(2,1)} fusion(f32[512,2560]{1,0:T(8,128)S(1)} %fusion.11, bf16[512,768]{1,0:T(8,128)(2,1)S(1)} %get-tuple-element.38, bf16[1,1,2560,768]{3,2,1,0:T(8,128)(2,1)S(1)} %copy-done.22), kind=kOutput, calls=%fused_computation | convolution fusion | flops 2015887360 | bytes 12582912 | tf_op jit(solution)/shard_map/dot_general | solution.py:201
  136.5 15.0 %all-to-all-done.3 = bf16[8,64,2560]{2,1,0:T(8,128)(2,1)S(1)} async-done(((bf16[8,64,2560]{2,1,0:T(8,128)(2,1)}), bf16[8,64,2560]{2,1,0:T(8,128)(2,1)S(1)}, u32[]{:S(2)}, u32[]{:S(2)}) %all-to-all-start.3) | async-done | bytes 2621472 | tf_op jit(solution)/shard_map/all_to_all | solution.py:239
  151.5 1.5 join_forward.1
  153.0 0.0 copy-start.9
  153.1 0.6 copy-done.9
  153.7 0.8 copy-done.11
  154.5 0.5 broadcast.11
  155.0 0.7 reduce.8
  155.7 0.1 reshape.61
  155.8 8.7 %all_to_all.35 = f32[8,1,64]{2,1,0:T(1,128)S(1)} all-to-all(f32[8,1,64]{2,1,0:T(1,128)S(1)} %bitcast.90), channel_id=1, replica_groups=mesh['section'=16,'expert'=8] {'expert'}, dimensions={0} | all-to-all | bytes 4096 | tf_op jit(solution)/shard_map/all_to_all | solution.py:301
  164.4 3.6 %all-to-all-start.4 = ((bf16[8,64,2560]{2,1,0:T(8,128)(2,1)}), bf16[8,64,2560]{2,1,0:T(8,128)(2,1)S(1)}, u32[]{:S(2)}, u32[]{:S(2)}) async-start(bf16[8,64,2560]{2,1,0:T(8,128)(2,1)} %bitcast.86), calls=%async_computation.4 | async-start | bytes 5242880 | tf_op jit(solution)/shard_map/all_to_all | solution.py:239
  168.1 1.9 collective-permute-start
  170.0 0.7 reduce.9
  170.7 0.1 mul.58
  170.8 7.0 %fusion.2 = bf16[1,1,768,2560]{3,2,1,0:T(8,128)(2,1)} fusion(bf16[512,2560]{1,0:T(8,128)(2,1)} %bitcast.13, f32[512,768]{1,0:T(8,128)} %copy-done.26, f32[512]{0:T(512)S(1)} %mul.58, f32[512,768]{1,0:T(8,128)} %fusion.13), kind=kOutput, calls=%fused_computation.6 | convolution fusion | flops 2018770944 | bytes 9701376 | tf_op jit(solution)/shard_map/dot_general | solution.py:195
  177.8 21.8 %all-to-all-done.4 = bf16[8,64,2560]{2,1,0:T(8,128)(2,1)S(1)} async-done(((bf16[8,64,2560]{2,1,0:T(8,128)(2,1)}), bf16[8,64,2560]{2,1,0:T(8,128)(2,1)S(1)}, u32[]{:S(2)}, u32[]{:S(2)}) %all-to-all-start.4) | async-done | bytes 2621472 | tf_op jit(solution)/shard_map/all_to_all | solution.py:239
  199.6 1.1 copy-done.3
  200.7 1.1 copy-done.5
  201.8 2.4 %join_backward.1 = (bf16[128,2560]{1,0:T(8,128)(2,1)}, f32[1,2560]{1,0:T(1,128)S(1)}) custom-call(s32[1]{0:T(128)} %bitcast.refs_0_, bf16[512,2560]{1,0:T(8,128)(2,1)S(1)} %bitcast.63, bf16[128,2560]{1,0:T(8,128)(2,1)S(1)} %bitcast.68, bf16[128,2560]{1,0:T(8,128)(2,1)S(1)} %bitcast.70, bf16[128,2560]{1,0:T(8,128)(2,1)S(1)} %bitcast.72, ...), custom_call_target="tpu_custom_call" | custom-call | tf_op jit(solution)/shard_map/join_backward/pallas_call | solution.py:183
  204.2 2.9 %collective-permute-start.1 = (bf16[128,2560]{1,0:T(8,128)(2,1)}, bf16[128,2560]{1,0:T(8,128)(2,1)S(1)}, u32[]{:S(2)}, u32[]{:S(2)}) collective-permute-start(bf16[128,2560]{1,0:T(8,128)(2,1)} %get-tuple-element.35), channel_id=1, source_target_pairs={{8,0},{16,8},{24,16},{32,24},{40,32},{48,40},{56,48},{64,56},{72,6... | collective-permute-start | bytes 1966088 | tf_op jit(solution)/shard_map/ppermute | solution.py:20
  207.0 4.3 %fusion = bf16[1,1,2560,768]{3,2,1,0:T(8,128)(2,1)} fusion(bf16[512,2560]{1,0:T(8,128)(2,1)S(1)} %bitcast.84, bf16[512,768]{1,0:T(8,128)(2,1)S(1)} %copy-done.24, f32[512]{0:T(512)S(1)} %mul.58), kind=kOutput, calls=%fused_computation.4 | convolution fusion | flops 2016411648 | bytes 7342080 | tf_op jit(solution)/shard_map/dot_general | solution.py:195
  211.3 0.7 broadcast_in_dim.41
  212.0 5.7 %all-to-all-start.5 = ((f32[8,1,2560]{2,1,0:T(1,128)}), f32[8,1,2560]{2,1,0:T(1,128)S(1)}, u32[]{:S(2)}, u32[]{:S(2)}) async-start(f32[8,1,2560]{2,1,0:T(1,128)} %broadcast_in_dim.41), calls=%async_computation.5 | async-start | bytes 163840 | tf_op jit(solution)/shard_map/all_to_all | solution.py:321
  217.7 5.4 %fusion.1 = bf16[1,1,2560,768]{3,2,1,0:T(8,128)(2,1)} fusion(bf16[512,2560]{1,0:T(8,128)(2,1)S(1)} %bitcast.85, bf16[512,768]{1,0:T(8,128)(2,1)} %copy-done.27, f32[512]{0:T(512)S(1)} %mul.58), kind=kOutput, calls=%fused_computation.5 | convolution fusion | flops 2016411648 | bytes 7342080 | tf_op jit(solution)/shard_map/dot_general | solution.py:195
  223.1 0.0 collective-permute-done
  223.1 1.0 all-to-all-done.5
  224.1 0.1 reduce_sum.11
  224.2 0.6 reduce_sum.12
  224.8 0.0 collective-permute-done.1
  224.8 2.0 copy.46
  226.8 0.8 copy.47
  (40 shorter events, 0.1 us)
Async XLA Ops:
  1.4 1.1 copy-start
  2.5 0.7 copy-start.6
  6.0 6.2 %copy-start.15 = (f32[2560]{0:T(1024)S(1)}, f32[2560]{0:T(1024)}, u32[]{:S(2)}) copy-start(f32[2560]{0:T(1024)} %param.24) | copy-start | bytes 30724
  6.0 6.2 %copy-start.16 = (s32[1,128,2]{1,2,0:T(2,128)S(1)}, s32[1,128,2]{1,2,0:T(2,128)}, u32[]{:S(2)}) copy-start(s32[1,128,2]{1,2,0:T(2,128)} %param.17) | copy-start | bytes 3076
  6.0 6.3 %copy-start.17 = (f32[1,128,2]{1,2,0:T(2,128)S(1)}, f32[1,128,2]{1,2,0:T(2,128)}, u32[]{:S(2)}) copy-start(f32[1,128,2]{1,2,0:T(2,128)} %param.18) | copy-start | bytes 3076
  6.0 6.4 %copy-start.18 = (f32[1,128,2]{1,2,0:T(2,128)S(1)}, f32[1,128,2]{1,2,0:T(2,128)}, u32[]{:S(2)}) copy-start(f32[1,128,2]{1,2,0:T(2,128)} %param.19) | copy-start | bytes 3076
  6.0 6.5 %copy-start.1 = (bf16[1,128,2560]{2,1,0:T(8,128)(2,1)S(1)}, bf16[1,128,2560]{2,1,0:T(8,128)(2,1)}, u32[]{:S(2)}) copy-start(bf16[1,128,2560]{2,1,0:T(8,128)(2,1)} %param.13) | copy-start | bytes 1966084
  6.0 6.5 %copy-start.2 = (bf16[1,128,2560]{2,1,0:T(8,128)(2,1)S(1)}, bf16[1,128,2560]{2,1,0:T(8,128)(2,1)}, u32[]{:S(2)}) copy-start(bf16[1,128,2560]{2,1,0:T(8,128)(2,1)} %param.14) | copy-start | bytes 1966084
  6.0 6.5 %copy-start.4 = (bf16[1,128,2560]{2,1,0:T(8,128)(2,1)S(1)}, bf16[1,128,2560]{2,1,0:T(8,128)(2,1)}, u32[]{:S(2)}) copy-start(bf16[1,128,2560]{2,1,0:T(8,128)(2,1)} %param.15) | copy-start | bytes 1966084
  6.1 6.5 %copy-start.7 = (f32[1,2560]{1,0:T(1,128)S(1)}, f32[1,2560]{1,0:T(1,128)}, u32[]{:S(2)}) copy-start(f32[1,2560]{1,0:T(1,128)} %refs_6_.1) | copy-start | bytes 30724
  6.1 38.8 %all-to-all-start = ((bf16[8,64,2560]{2,1,0:T(8,128)(2,1)}), bf16[8,64,2560]{2,1,0:T(8,128)(2,1)}, u32[]{:S(2)}, u32[]{:S(2)}) async-start(bf16[8,64,2560]{2,1,0:T(8,128)(2,1)} %bitcast.3), calls=%async_computation | async-start | bytes 5242880 | tf_op jit(solution)/shard_map/all_to_all | solution.py:239
  44.9 3.8 %copy-start.19 = (s32[128]{0:T(128)S(1)}, s32[128]{0:T(128)}, u32[]{:S(2)}) copy-start(s32[128]{0:T(128)} %param.25) | copy-start | bytes 1540
  44.9 35.6 %all-to-all-start.1 = ((bf16[8,64,2560]{2,1,0:T(8,128)(2,1)}), bf16[8,64,2560]{2,1,0:T(8,128)(2,1)S(1)}, u32[]{:S(2)}, u32[]{:S(2)}) async-start(bf16[8,64,2560]{2,1,0:T(8,128)(2,1)} %bitcast.10), calls=%async_computation.1 | async-start | bytes 5242880 | tf_op jit(solution)/shard_map/all_to_all | solution.py:239
  80.5 22.3 %copy-start.12 = (bf16[8,64,2560]{2,1,0:T(8,128)(2,1)}, bf16[8,64,2560]{2,1,0:T(8,128)(2,1)S(1)}, u32[]{:S(2)}) copy-start(bf16[8,64,2560]{2,1,0:T(8,128)(2,1)S(1)} %all-to-all-done.1) | copy-start | bytes 7864324
  80.5 35.6 %all-to-all-start.2 = ((bf16[8,64,2560]{2,1,0:T(8,128)(2,1)}), bf16[8,64,2560]{2,1,0:T(8,128)(2,1)}, u32[]{:S(2)}, u32[]{:S(2)}) async-start(bf16[8,64,2560]{2,1,0:T(8,128)(2,1)} %bitcast.87), calls=%async_computation.2 | async-start | bytes 5242880 | tf_op jit(solution)/shard_map/all_to_all | solution.py:239
  116.0 35.5 %all-to-all-start.3 = ((bf16[8,64,2560]{2,1,0:T(8,128)(2,1)}), bf16[8,64,2560]{2,1,0:T(8,128)(2,1)S(1)}, u32[]{:S(2)}, u32[]{:S(2)}) async-start(bf16[8,64,2560]{2,1,0:T(8,128)(2,1)} %bitcast.88), calls=%async_computation.3 | async-start | bytes 5242880 | tf_op jit(solution)/shard_map/all_to_all | solution.py:239
  119.9 5.3 %copy-start.20 = (bf16[1,1,768,2560]{3,2,1,0:T(8,128)(2,1)S(1)}, bf16[1,1,768,2560]{3,2,1,0:T(8,128)(2,1)}, u32[]{:S(2)}) copy-start(bf16[1,1,768,2560]{3,2,1,0:T(8,128)(2,1)} %param.22) | copy-start | bytes 11796484
  119.9 5.3 %copy-start.25 = (f32[512,768]{1,0:T(8,128)S(1)}, f32[512,768]{1,0:T(8,128)}, u32[]{:S(2)}) copy-start(f32[512,768]{1,0:T(8,128)} %fusion.13) | copy-start | bytes 4718596
  125.2 4.9 %copy-start.26 = (f32[512,768]{1,0:T(8,128)}, f32[512,768]{1,0:T(8,128)S(1)}, u32[]{:S(2)}) copy-start(f32[512,768]{1,0:T(8,128)S(1)} %fusion.7) | copy-start | bytes 4718596
  125.2 5.0 %copy-start.21 = (bf16[1,1,2560,768]{3,2,1,0:T(8,128)(2,1)S(1)}, bf16[1,1,2560,768]{3,2,1,0:T(8,128)(2,1)}, u32[]{:S(2)}) copy-start(bf16[1,1,2560,768]{3,2,1,0:T(8,128)(2,1)} %param.20) | copy-start | bytes 11796484
  130.1 2.3 %copy-start.23 = (bf16[512,768]{1,0:T(8,128)(2,1)}, bf16[512,768]{1,0:T(8,128)(2,1)S(1)}, u32[]{:S(2)}) copy-start(bf16[512,768]{1,0:T(8,128)(2,1)S(1)} %get-tuple-element.39) | copy-start | bytes 2359300
  130.1 2.3 %copy-start.27 = (bf16[512,768]{1,0:T(8,128)(2,1)}, bf16[512,768]{1,0:T(8,128)(2,1)S(1)}, u32[]{:S(2)}) copy-start(bf16[512,768]{1,0:T(8,128)(2,1)S(1)} %get-tuple-element.38) | copy-start | bytes 2359300
  130.1 2.7 %copy-start.22 = (bf16[1,1,2560,768]{3,2,1,0:T(8,128)(2,1)S(1)}, bf16[1,1,2560,768]{3,2,1,0:T(8,128)(2,1)}, u32[]{:S(2)}) copy-start(bf16[1,1,2560,768]{3,2,1,0:T(8,128)(2,1)} %param.21) | copy-start | bytes 11796484
  153.0 0.6 copy-start.9
  153.7 0.8 copy-start.11
  164.4 35.2 %all-to-all-start.4 = ((bf16[8,64,2560]{2,1,0:T(8,128)(2,1)}), bf16[8,64,2560]{2,1,0:T(8,128)(2,1)S(1)}, u32[]{:S(2)}, u32[]{:S(2)}) async-start(bf16[8,64,2560]{2,1,0:T(8,128)(2,1)} %bitcast.86), calls=%async_computation.4 | async-start | bytes 5242880 | tf_op jit(solution)/shard_map/all_to_all | solution.py:239
  168.1 55.0 %collective-permute-start = (bf16[128,2560]{1,0:T(8,128)(2,1)}, bf16[128,2560]{1,0:T(8,128)(2,1)}, u32[]{:S(2)}, u32[]{:S(2)}) collective-permute-start(bf16[128,2560]{1,0:T(8,128)(2,1)} %copy-done.11), channel_id=1, source_target_pairs={{0,8},{8,16},{16,24},{24,32},{32,40},{40,48},{48,56},{56,64},{64,7... | collective-permute-start | bytes 1966088 | tf_op jit(solution)/shard_map/ppermute | solution.py:20
  170.8 28.8 %copy-start.8 = (f32[1,2560]{1,0:T(1,128)S(1)}, f32[1,2560]{1,0:T(1,128)}, u32[]{:S(2)}) copy-start(f32[1,2560]{1,0:T(1,128)} %refs_6_.1) | copy-start | bytes 30724
  170.8 28.8 %copy-start.10 = (f32[128,1]{1,0:T(8,128)S(1)}, f32[128,1]{1,0:T(8,128)}, u32[]{:S(2)}) copy-start(f32[128,1]{1,0:T(8,128)} %copy-done.9) | copy-start | bytes 1540
  199.6 1.1 copy-start.3
  200.7 1.1 copy-start.5
  201.8 5.2 %copy-start.13 = (bf16[8,64,2560]{2,1,0:T(8,128)(2,1)S(1)}, bf16[8,64,2560]{2,1,0:T(8,128)(2,1)}, u32[]{:S(2)}) copy-start(bf16[8,64,2560]{2,1,0:T(8,128)(2,1)} %copy-done.12) | copy-start | bytes 7864324
  201.8 5.3 %copy-start.24 = (bf16[512,768]{1,0:T(8,128)(2,1)S(1)}, bf16[512,768]{1,0:T(8,128)(2,1)}, u32[]{:S(2)}) copy-start(bf16[512,768]{1,0:T(8,128)(2,1)} %copy-done.23) | copy-start | bytes 2359300
  204.2 13.5 %copy-start.14 = (bf16[8,64,2560]{2,1,0:T(8,128)(2,1)S(1)}, bf16[8,64,2560]{2,1,0:T(8,128)(2,1)}, u32[]{:S(2)}) copy-start(bf16[8,64,2560]{2,1,0:T(8,128)(2,1)} %copy-done.12) | copy-start | bytes 7864324
  204.2 20.6 %collective-permute-start.1 = (bf16[128,2560]{1,0:T(8,128)(2,1)}, bf16[128,2560]{1,0:T(8,128)(2,1)S(1)}, u32[]{:S(2)}, u32[]{:S(2)}) collective-permute-start(bf16[128,2560]{1,0:T(8,128)(2,1)} %get-tuple-element.35), channel_id=1, source_target_pairs={{8,0},{16,8},{24,16},{32,24},{40,32},{48,40},{56,48},{64,56},{72,6... | collective-permute-start | bytes 1966088 | tf_op jit(solution)/shard_map/ppermute | solution.py:20
  212.0 12.1 %all-to-all-start.5 = ((f32[8,1,2560]{2,1,0:T(1,128)}), f32[8,1,2560]{2,1,0:T(1,128)S(1)}, u32[]{:S(2)}, u32[]{:S(2)}) async-start(f32[8,1,2560]{2,1,0:T(1,128)} %broadcast_in_dim.41), calls=%async_computation.5 | async-start | bytes 163840 | tf_op jit(solution)/shard_map/all_to_all | solution.py:321
where the time goes:
time: 229 us; the launch traced here: 228 us
  waiting for transfers between devices  104 us (45%)
  matrix products  56.1 us (24%)
  starting transfers between devices  32.1 us (14%)
  Pallas kernels  12.1 us (5%)
  local copies, waits for them, and re-layouts  11.9 us (5%)
  blocking collectives  8.68 us (4%)
    all_to_all x5, waiting for transfers between devices, exchange(): lax.all_to_all(value.reshape(groups, capacity, width), 'expert', split_ax...  103 us
    all_to_all x5, starting transfers between devices, exchange(): lax.all_to_all(value.reshape(groups, capacity, width), 'expert', split_ax...  21.7 us
    dot_general x3, matrix products, contract_rows(): lax.dot_general(left_op, right_op, (((0,), (0,)), ((), ())), preferred_el...  16.7 us
    pallas_call x4, Pallas kernels, call(): pl.pallas_call(kernel, out_shape=[jax.ShapeDtypeStruct(shape, dtype) for...  12.1 us
    dot_general x1, matrix products, on_device(): out_f = jnp.dot(hidden_f, wd, preferred_element_type=f32).astype(bf16)  11.6 us
    dot_general x3, matrix products, contract_cols(): lax.dot_general(left_op, right_op, (((1,), (1,)), ((), ())), preferred_el...  10.9 us
    unnamed x62, local copies, waits for them, and re-layouts  9.85 us
    all_to_all x1, blocking collectives, on_device(): lax.all_to_all(coef_slots.reshape(groups, 1, capacity), 'expert', split_a...  8.68 us
  transfers between devices with their start and end apart: 8, of which 6 were waited for; matrix products, arithmetic and copies ran while one was open for 26% of the time, Pallas kernels for 3%

commit v1 on v0

--- a/solution.py
+++ b/solution.py
@@ -83,8 +83,7 @@
     back_ids_ref,
     fwd_gates_ref,
     back_gates_ref,
-    rows_ref,
-    dout_ref,
+    out_ref,
 ):
     is_last = last_ref[0] == 1
     ids = jnp.where(is_last, fwd_ids_ref[...], back_ids_ref[...])
@@ -95,14 +94,14 @@
     x = jnp.where(is_last, fwd_ref[...].astype(f32), back_ref[...].astype(f32))
     normed = (x * inv_rms_of(x) * gain_ref[...]).astype(bf16)
     for cols in chunks(x.shape[1]):
-        rows_ref[:, cols] = over_tokens(pick, normed[:, cols]).astype(bf16)
+        out_ref[:, cols] = over_tokens(pick, normed[:, cols]).astype(bf16)
         cot = cot_ref[:, cols]
         head = jnp.broadcast_to(head_ref[:, cols], cot.shape)
         head_high = head.astype(bf16)
         head_low = (head - head_high.astype(f32)).astype(bf16)
         cot_high = jnp.where(is_last, head_high.astype(f32), cot.astype(f32)).astype(bf16)
         cot_low = jnp.where(is_last, head_low.astype(f32), 0.0).astype(bf16)
-        dout_ref[:, cols] = (
+        out_ref[:, slice(cols.start + x.shape[1], cols.stop + x.shape[1])] = (
             over_tokens(high, cot_high) + over_tokens(low, cot_high) + over_tokens(high, cot_low)
         ).astype(bf16)
 
@@ -237,9 +236,13 @@
 
     def exchange(value):
         out = lax.all_to_all(
-            value.reshape(groups, capacity, width), "expert", split_axis=0, concat_axis=0, tiled=True
+            value.reshape(groups, capacity, value.shape[1]),
+            "expert",
+            split_axis=0,
+            concat_axis=0,
+            tiled=True,
         )
-        return out.reshape(slots, width)
+        return out.reshape(value.shape)
 
     (send_f,) = call(
         bind(send_forward),
@@ -249,10 +252,10 @@
         [vmem] * 3,
     )
     rows_f = exchange(send_f)
-    send_b, send_d = call(
+    (send_b,) = call(
         bind(send_backward),
         "send_backward",
-        [((slots, width), bf16)] * 2,
+        [((slots, 2 * width), bf16)],
         (
             last,
             x_fwd,
@@ -267,17 +270,16 @@
         ),
         [smem] + [vmem] * 9,
     )
-    rows_f, send_b, send_d = lax.optimization_barrier((rows_f, send_b, send_d))
-    rows_b = exchange(send_b)
+    rows_f, send_b = lax.optimization_barrier((rows_f, send_b))
+    rows_bd = exchange(send_b)
     gate_pre = jnp.dot(rows_f, wg, preferred_element_type=f32)
     up_pre = jnp.dot(rows_f, wu, preferred_element_type=f32)
     hidden_f = (jax.nn.silu(gate_pre) * up_pre).astype(bf16)
     out_f = jnp.dot(hidden_f, wd, preferred_element_type=f32).astype(bf16)
-    rows_b, send_d = lax.optimization_barrier((rows_b, send_d))
-    rows_d = exchange(send_d)
-    rows_d, out_f = lax.optimization_barrier((rows_d, out_f))
+    rows_bd, out_f = lax.optimization_barrier((rows_bd, out_f))
     ret_f = exchange(out_f)
 
+    rows_b, rows_d = rows_bd[:, :width], rows_bd[:, width:]
     gate_pre = jnp.dot(rows_b, wg, preferred_element_type=f32)
     up_pre = jnp.dot(rows_b, wu, preferred_element_type=f32)
     sig = jax.nn.sigmoid(gate_pre)
@@ -297,10 +299,16 @@
         (last, ret_f, x_fwd, fwd_routes[0], fwd_gates[0], head, verdict_labels[:, None]),
         [smem] + [vmem] * 6,
     )
+    mine = lax.axis_index("expert")
+    table = jnp.where(jnp.arange(groups)[:, None] == mine, coef_slots, 0.0)
+    step = 1
+    while step < groups:
+        table = table + lax.ppermute(
+            table, "expert", [(source, source ^ step) for source in range(groups)]
+        )
+        step *= 2
     next_input = passed_along(layer_out, "section", 1)
-    coef_rows = lax.all_to_all(
-        coef_slots.reshape(groups, 1, capacity), "expert", split_axis=0, concat_axis=0, tiled=True
-    ).reshape(slots, 1)
+    coef_rows = lax.dynamic_slice_in_dim(table, mine * capacity, capacity, axis=1).reshape(slots, 1)
 
     def scaled(value):
         return (value.astype(f32) * coef_rows).astype(bf16)
@@ -309,6 +317,9 @@
     grad_g = contract_rows(rows_b, scaled(d_gate)).astype(bf16)
     grad_u = contract_rows(rows_b, scaled(d_up)).astype(bf16)
 
+    ret_d, next_input, grad_d, grad_g, grad_u = lax.optimization_barrier(
+        (ret_d, next_input, grad_d, grad_g, grad_u)
+    )
     d_input, gain_local = call(
         bind(join_backward),
         "join_backward",

time: 229 us -> 235 us (1.026)
  waiting for transfers between devices: 104 us -> 115 us
  blocking collectives: 8.68 us -> 0 us
  starting transfers between devices: 32.1 us -> 35.9 us
    ppermute x0 -> x3, waiting for transfers between devices: none -> 27.8 us  [on_device(): lax.ppermute(table, 'expert', [(source, source ^ step) for source in rang...]
    all_to_all x5 -> x4, waiting for transfers between devices: 103 us -> 80.6 us  [exchange(): lax.all_to_all(value.reshape(groups, capacity, value.shape[1]), 'expert',...]
    all_to_all x1 -> x0, blocking collectives: 8.68 us -> none  [on_device(): lax.all_to_all(coef_slots.reshape(groups, 1, capacity), 'expert', split_a...]
    all_to_all x1, waiting for transfers between devices: 1.02 us -> 6.36 us  [on_device(): lax.all_to_all(jnp.broadcast_to(gain_local[None], (groups, 1, width)), 'e...]
    ppermute x0 -> x3, starting transfers between devices: none -> 5.21 us  [on_device(): lax.ppermute(table, 'expert', [(source, source ^ step) for source in rang...]
    ppermute x2, starting transfers between devices: 4.77 us -> 9.01 us  [passed_along(): lax.ppermute(value, axis, [(source, source + steps) for source in range(i...]
    all_to_all x5 -> x4, starting transfers between devices: 21.7 us -> 18.3 us  [exchange(): lax.all_to_all(value.reshape(groups, capacity, value.shape[1]), 'expert',...]
    unnamed x62 -> x64, local copies, waits for them, and re-layouts: 9.85 us -> 12.7 us
  transfers between devices with their start and end apart: 8 -> 10, of which waited for: 6 -> 7; matrix products, arithmetic and copies ran while one was open for 26% -> 25% of each run, Pallas kernels for 3% -> 3%
where the time goes in v1:
time: 235 us; the launch traced here: 234 us
  waiting for transfers between devices  115 us (49%)
  matrix products  55.4 us (24%)
  starting transfers between devices  35.9 us (15%)
  local copies, waits for them, and re-layouts  14.2 us (6%)
  Pallas kernels  12.5 us (5%)
    all_to_all x4, waiting for transfers between devices, exchange(): lax.all_to_all(value.reshape(groups, capacity, value.shape[1]), 'expert',...  80.6 us
    ppermute x3, waiting for transfers between devices, on_device(): lax.ppermute(table, 'expert', [(source, source ^ step) for source in rang...  27.8 us
    dot_general x3, matrix products, contract_rows(): lax.dot_general(left_op, right_op, (((0,), (0,)), ((), ())), preferred_el...  18.5 us
    all_to_all x4, starting transfers between devices, exchange(): lax.all_to_all(value.reshape(groups, capacity, value.shape[1]), 'expert',...  18.3 us
    unnamed x64, local copies, waits for them, and re-layouts  12.7 us
    pallas_call x4, Pallas kernels, call(): pl.pallas_call(kernel, out_shape=[jax.ShapeDtypeStruct(shape, dtype) for...  12.5 us
    dot_general x1, matrix products, on_device(): out_f = jnp.dot(hidden_f, wd, preferred_element_type=f32).astype(bf16)  11.2 us
    dot_general x3, matrix products, contract_cols(): lax.dot_general(left_op, right_op, (((1,), (1,)), ((), ())), preferred_el...  10.9 us
  transfers between devices with their start and end apart: 10, of which 7 were waited for; matrix products, arithmetic and copies ran while one was open for 25% of the time, Pallas kernels for 3%

profile of v1, /device:TPU:4, one launch (start us, length us, event | category | flops | bytes accessed | tf_op | source)
XLA Modules:
  0.0 234.2 jit_solution(4830007933325982898)
XLA Ops:
  0.6 0.8 copy.29
  1.4 1.1 copy-done
  2.5 0.7 copy-done.8
  3.2 2.8 %send_forward.1 = bf16[512,2560]{1,0:T(8,128)(2,1)} custom-call(bf16[128,2560]{1,0:T(8,128)(2,1)S(1)} %bitcast.52, f32[1,2560]{1,0:T(1,128)S(1)} %copy-done.8, s32[128,2]{1,0:T(8,128)S(1)} %bitcast.62), custom_call_target="tpu_custom_call" | custom-call | tf_op jit(solution)/shard_map/send_forward/pallas_call | solution.py:182
  6.0 0.0 copy-start.1
  6.0 0.0 copy-start.4
  6.0 0.0 copy-start.6
  6.1 0.0 copy-start.9
  6.1 6.1 %all-to-all-start = ((bf16[8,64,2560]{2,1,0:T(8,128)(2,1)}), bf16[8,64,2560]{2,1,0:T(8,128)(2,1)}, u32[]{:S(2)}, u32[]{:S(2)}) async-start(bf16[8,64,2560]{2,1,0:T(8,128)(2,1)} %bitcast.2), calls=%async_computation | async-start | bytes 5242880 | tf_op jit(solution)/shard_map/all_to_all | solution.py:238
  12.2 0.1 copy.30
  12.3 0.1 copy.31
  12.4 0.1 copy.32
  12.6 5.8 %send_backward.1 = bf16[512,5120]{1,0:T(8,128)(2,1)} custom-call(s32[1]{0:T(128)} %bitcast.4.refs_0_, bf16[128,2560]{1,0:T(8,128)(2,1)S(1)} %bitcast.53, bf16[128,2560]{1,0:T(8,128)(2,1)S(1)} %bitcast.58, bf16[128,2560]{1,0:T(8,128)(2,1)S(1)} %bitcast.60, f32[1,2560]{1,0:T(1,128)S(1)} %copy-done.9, f32[1,2560]{1,0:T(1,128)S(1)} %broadcast_in_dim.59.refs_5_.refs_7_, ...), custom_call_target="tpu_custom_call" | custom-call | tf_op jit(solution)/shard_map/send_backward/pallas_call | solution.py:182
  18.4 26.4 %all-to-all-done = bf16[8,64,2560]{2,1,0:T(8,128)(2,1)} async-done(((bf16[8,64,2560]{2,1,0:T(8,128)(2,1)}), bf16[8,64,2560]{2,1,0:T(8,128)(2,1)}, u32[]{:S(2)}, u32[]{:S(2)}) %all-to-all-start) | async-done | bytes 2621472 | tf_op jit(solution)/shard_map/all_to_all | solution.py:238
  44.9 4.8 %all-to-all-start.1 = ((bf16[8,64,5120]{2,1,0:T(8,128)(2,1)}), bf16[8,64,5120]{2,1,0:T(8,128)(2,1)}, u32[]{:S(2)}, u32[]{:S(2)}) async-start(bf16[8,64,5120]{2,1,0:T(8,128)(2,1)} %bitcast.74), calls=%async_computation.1 | async-start | bytes 10485760 | tf_op jit(solution)/shard_map/all_to_all | solution.py:238
  49.7 0.1 copy.33.refs_6_
  49.8 5.1 %fusion.12 = f32[512,768]{1,0:T(8,128)S(1)} fusion(bf16[512,2560]{1,0:T(8,128)(2,1)} %bitcast.3, bf16[1,1,2560,768]{3,2,1,0:T(8,128)(2,1)} %param.20), kind=kOutput, calls=%fused_computation.17 | convolution fusion | flops 2013265920 | bytes 8126464 | tf_op jit(solution)/shard_map/dot_general | solution.py:275
  54.9 11.2 %convolution_convert_fusion.3 = bf16[512,2560]{1,0:T(8,128)(2,1)} fusion(bf16[1,1,768,2560]{3,2,1,0:T(8,128)(2,1)} %param.22, f32[512,768]{1,0:T(8,128)S(1)} %fusion.12, bf16[512,2560]{1,0:T(8,128)(2,1)} %bitcast.3, bf16[1,1,2560,768]{3,2,1,0:T(8,128)(2,1)} %param.21), kind=kOutput, calls=%fused_computation.4 | convolution fusion | flops 4030201856 | bytes 14680064 | tf_op jit(solution)/shard_map/dot_general | solution.py:278
  66.1 43.4 %all-to-all-done.1 = bf16[8,64,5120]{2,1,0:T(8,128)(2,1)} async-done(((bf16[8,64,5120]{2,1,0:T(8,128)(2,1)}), bf16[8,64,5120]{2,1,0:T(8,128)(2,1)}, u32[]{:S(2)}, u32[]{:S(2)}) %all-to-all-start.1) | async-done | bytes 5242912 | tf_op jit(solution)/shard_map/all_to_all | solution.py:238
  109.4 3.8 %all-to-all-start.2 = ((bf16[8,64,2560]{2,1,0:T(8,128)(2,1)}), bf16[8,64,2560]{2,1,0:T(8,128)(2,1)S(1)}, u32[]{:S(2)}, u32[]{:S(2)}) async-start(bf16[8,64,2560]{2,1,0:T(8,128)(2,1)} %bitcast.76), calls=%async_computation.2 | async-start | bytes 5242880 | tf_op jit(solution)/shard_map/all_to_all | solution.py:238
  113.3 0.0 copy-start.21
  113.3 5.2 %fusion.10 = f32[512,768]{1,0:T(8,128)S(1)} fusion(bf16[1,1,2560,768]{3,2,1,0:T(8,128)(2,1)} %param.20, bf16[512,5120]{1,0:T(8,128)(2,1)} %bitcast.11), kind=kOutput, calls=%fused_computation.15 | convolution fusion | flops 2013265920 | bytes 8126464 | tf_op jit(solution)/shard_map/dot_general | solution.py:283
  118.5 0.0 copy-start.19
  118.6 4.5 %fusion.4 = f32[512,768]{1,0:T(8,128)S(1)} fusion(bf16[1,1,2560,768]{3,2,1,0:T(8,128)(2,1)S(1)} %copy-done.21, bf16[512,5120]{1,0:T(8,128)(2,1)} %bitcast.11), kind=kOutput, calls=%fused_computation.9 | convolution fusion | flops 2013265920 | bytes 8126464 | tf_op jit(solution)/shard_map/dot_general | solution.py:284
  123.1 0.0 copy-start.20
  123.1 4.9 %multiply_convert_fusion.4 = (bf16[512,768]{1,0:T(8,128)(2,1)S(1)}, bf16[512,768]{1,0:T(8,128)(2,1)S(1)}) fusion(f32[512,768]{1,0:T(8,128)S(1)} %fusion.10, f32[512,768]{1,0:T(8,128)S(1)} %fusion.4, bf16[1,1,768,2560]{3,2,1,0:T(8,128)(2,1)S(1)} %copy-done.19, bf16[512,5120]{1,0:T(8,128)(2,1)} %bitcast.11), kind=kOutput, calls=%fused_computation.29 | convolution fusion | flops 2018377728 | bytes 11272192 | tf_op jit(solution)/shard_map/dot_general | solution.py:200
  128.1 0.0 copy-start.22
  128.1 2.2 fusion.8
  130.4 3.7 %add_convert_fusion = bf16[512,2560]{1,0:T(8,128)(2,1)} fusion(f32[512,2560]{1,0:T(8,128)S(1)} %fusion.8, bf16[512,768]{1,0:T(8,128)(2,1)S(1)} %get-tuple-element.38, bf16[1,1,2560,768]{3,2,1,0:T(8,128)(2,1)S(1)} %copy-done.21), kind=kOutput, calls=%fused_computation | convolution fusion | flops 2015887360 | bytes 12582912 | tf_op jit(solution)/shard_map/dot_general | solution.py:200
  134.1 10.8 %all-to-all-done.2 = bf16[8,64,2560]{2,1,0:T(8,128)(2,1)S(1)} async-done(((bf16[8,64,2560]{2,1,0:T(8,128)(2,1)}), bf16[8,64,2560]{2,1,0:T(8,128)(2,1)S(1)}, u32[]{:S(2)}, u32[]{:S(2)}) %all-to-all-start.2) | async-done | bytes 2621472 | tf_op jit(solution)/shard_map/all_to_all | solution.py:238
  144.9 1.5 copy-done.2
  146.4 3.6 %all-to-all-start.3 = ((bf16[8,64,2560]{2,1,0:T(8,128)(2,1)}), bf16[8,64,2560]{2,1,0:T(8,128)(2,1)S(1)}, u32[]{:S(2)}, u32[]{:S(2)}) async-start(bf16[8,64,2560]{2,1,0:T(8,128)(2,1)} %bitcast.75), calls=%async_computation.3 | async-start | bytes 5242880 | tf_op jit(solution)/shard_map/all_to_all | solution.py:238
  150.0 0.0 copy-start.3
  150.0 1.7 copy-done.3
  151.8 1.5 join_forward.1
  153.3 0.0 copy-start.11
  153.3 0.6 copy-done.11
  153.9 0.8 copy-done.13
  154.7 0.1 broadcast_select_fusion
  154.8 1.9 collective-permute-start.1
  156.7 24.3 %collective-permute-done.1 = f32[8,512]{1,0:T(8,128)S(1)} collective-permute-done((f32[8,512]{1,0:T(8,128)S(1)}, f32[8,512]{1,0:T(8,128)S(1)}, u32[]{:S(2)}, u32[]{:S(2)}) %collective-permute-start.1) | collective-permute-done | bytes 16416 | tf_op jit(solution)/shard_map/ppermute | solution.py:306
  181.0 0.1 fusion.29
  181.1 0.6 collective-permute-start.2
  181.6 3.2 %collective-permute-done.2 = f32[8,512]{1,0:T(8,128)S(1)} collective-permute-done((f32[8,512]{1,0:T(8,128)S(1)}, f32[8,512]{1,0:T(8,128)S(1)}, u32[]{:S(2)}, u32[]{:S(2)}) %collective-permute-start.2) | collective-permute-done | bytes 16416 | tf_op jit(solution)/shard_map/ppermute | solution.py:306
  184.8 0.1 fusion.36
  184.9 2.7 %collective-permute-start.3 = (f32[8,512]{1,0:T(8,128)S(1)}, f32[8,512]{1,0:T(8,128)S(1)}, u32[]{:S(2)}, u32[]{:S(2)}) collective-permute-start(f32[8,512]{1,0:T(8,128)S(1)} %fusion.36), channel_id=1, source_target_pairs={{0,4},{1,5},{2,6},{3,7},{4,0},{5,1},{6,2},{7,3},{8,12},{9,13},{10,... | collective-permute-start | bytes 49160 | tf_op jit(solution)/shard_map/ppermute | solution.py:306
  187.6 2.1 collective-permute-start
  189.7 0.4 collective-permute-done.3
  190.1 0.1 dynamic-slice_add_fusion
  190.2 0.1 mul.63
  190.3 6.2 %convolution_convert_fusion.1 = bf16[2560,768]{1,0:T(8,128)(2,1)} fusion(bf16[512,5120]{1,0:T(8,128)(2,1)} %bitcast.11, bf16[512,768]{1,0:T(8,128)(2,1)} %copy-done.22, f32[512]{0:T(512)S(1)} %mul.63), kind=kOutput, calls=%fused_computation.2 | convolution fusion | flops 2016411648 | bytes 7342080 | tf_op jit(solution)/shard_map/dot_general | solution.py:194
  196.5 6.1 %convolution_convert_fusion = bf16[2560,768]{1,0:T(8,128)(2,1)} fusion(bf16[512,5120]{1,0:T(8,128)(2,1)} %bitcast.11, bf16[512,768]{1,0:T(8,128)(2,1)S(1)} %copy-done.28, f32[512]{0:T(512)S(1)} %mul.63), kind=kOutput, calls=%fused_computation.1 | convolution fusion | flops 2016411648 | bytes 7342080 | tf_op jit(solution)/shard_map/dot_general | solution.py:194
  202.7 6.1 %convolution_convert_fusion.2 = bf16[768,2560]{1,0:T(8,128)(2,1)} fusion(bf16[512,5120]{1,0:T(8,128)(2,1)} %bitcast.11, f32[512,768]{1,0:T(8,128)S(1)} %copy-done.26, f32[512]{0:T(512)S(1)} %mul.63, f32[512,768]{1,0:T(8,128)S(1)} %copy-done.24), kind=kOutput, calls=%fused_computation.3 | convolution fusion | flops 2018770944 | bytes 9701376 | tf_op jit(solution)/shard_map/dot_general | solution.py:194
  208.8 1.1 copy-done.5
  209.9 1.1 copy-done.7
  211.0 2.4 %join_backward.1 = (bf16[128,2560]{1,0:T(8,128)(2,1)}, f32[1,2560]{1,0:T(1,128)S(1)}) custom-call(s32[1]{0:T(128)} %bitcast.4.refs_0_, bf16[512,2560]{1,0:T(8,128)(2,1)S(1)} %bitcast.56, bf16[128,2560]{1,0:T(8,128)(2,1)S(1)} %bitcast.55, bf16[128,2560]{1,0:T(8,128)(2,1)S(1)} %bitcast.59, bf16[128,2560]{1,0:T(8,128)(2,1)S(1)} %bitcast.61, ...), custom_call_target="tpu_custom_call" | custom-call | tf_op jit(solution)/shard_map/join_backward/pallas_call | solution.py:182
  213.4 6.9 %collective-permute-start.4 = (bf16[128,2560]{1,0:T(8,128)(2,1)}, bf16[128,2560]{1,0:T(8,128)(2,1)S(1)}, u32[]{:S(2)}, u32[]{:S(2)}) collective-permute-start(bf16[128,2560]{1,0:T(8,128)(2,1)} %get-tuple-element.33), channel_id=1, source_target_pairs={{8,0},{16,8},{24,16},{32,24},{40,32},{48,40},{56,48},{64,56},{72,6... | collective-permute-start | bytes 1966088 | tf_op jit(solution)/shard_map/ppermute | solution.py:20
  220.3 0.7 broadcast_in_dim.68
  221.0 3.4 %all-to-all-start.4 = ((f32[8,1,2560]{2,1,0:T(1,128)}), f32[8,1,2560]{2,1,0:T(1,128)S(1)}, u32[]{:S(2)}, u32[]{:S(2)}) async-start(f32[8,1,2560]{2,1,0:T(1,128)} %broadcast_in_dim.68), calls=%async_computation.4 | async-start | bytes 163840 | tf_op jit(solution)/shard_map/all_to_all | solution.py:332
  224.3 6.4 %all-to-all-done.4 = f32[8,1,2560]{2,1,0:T(1,128)S(1)} async-done(((f32[8,1,2560]{2,1,0:T(1,128)}), f32[8,1,2560]{2,1,0:T(1,128)S(1)}, u32[]{:S(2)}, u32[]{:S(2)}) %all-to-all-start.4) | async-done | bytes 81952 | tf_op jit(solution)/shard_map/all_to_all | solution.py:332
  230.7 0.1 reduce_sum.11
  230.8 0.6 reduce_sum.12
  231.4 2.0 copy.38
  233.3 0.8 copy.39
  (46 shorter events, 0.1 us)
Async XLA Ops:
  1.4 1.1 copy-start
  2.5 0.7 copy-start.8
  6.0 6.2 %copy-start.14 = (f32[2560]{0:T(1024)S(1)}, f32[2560]{0:T(1024)}, u32[]{:S(2)}) copy-start(f32[2560]{0:T(1024)} %param.24) | copy-start | bytes 30724
  6.0 6.2 %copy-start.15 = (s32[1,128,2]{1,2,0:T(2,128)S(1)}, s32[1,128,2]{1,2,0:T(2,128)}, u32[]{:S(2)}) copy-start(s32[1,128,2]{1,2,0:T(2,128)} %param.17) | copy-start | bytes 3076
  6.0 6.3 %copy-start.16 = (f32[1,128,2]{1,2,0:T(2,128)S(1)}, f32[1,128,2]{1,2,0:T(2,128)}, u32[]{:S(2)}) copy-start(f32[1,128,2]{1,2,0:T(2,128)} %param.18) | copy-start | bytes 3076
  6.0 6.4 %copy-start.17 = (f32[1,128,2]{1,2,0:T(2,128)S(1)}, f32[1,128,2]{1,2,0:T(2,128)}, u32[]{:S(2)}) copy-start(f32[1,128,2]{1,2,0:T(2,128)} %param.19) | copy-start | bytes 3076
  6.0 6.5 %copy-start.1 = (bf16[1,128,2560]{2,1,0:T(8,128)(2,1)S(1)}, bf16[1,128,2560]{2,1,0:T(8,128)(2,1)}, u32[]{:S(2)}) copy-start(bf16[1,128,2560]{2,1,0:T(8,128)(2,1)} %param.13) | copy-start | bytes 1966084
  6.0 6.5 %copy-start.4 = (bf16[1,128,2560]{2,1,0:T(8,128)(2,1)S(1)}, bf16[1,128,2560]{2,1,0:T(8,128)(2,1)}, u32[]{:S(2)}) copy-start(bf16[1,128,2560]{2,1,0:T(8,128)(2,1)} %param.14) | copy-start | bytes 1966084
  6.0 6.5 %copy-start.6 = (bf16[1,128,2560]{2,1,0:T(8,128)(2,1)S(1)}, bf16[1,128,2560]{2,1,0:T(8,128)(2,1)}, u32[]{:S(2)}) copy-start(bf16[1,128,2560]{2,1,0:T(8,128)(2,1)} %param.15) | copy-start | bytes 1966084
  6.1 6.5 %copy-start.9 = (f32[1,2560]{1,0:T(1,128)S(1)}, f32[1,2560]{1,0:T(1,128)}, u32[]{:S(2)}) copy-start(f32[1,2560]{1,0:T(1,128)} %refs_6_.1) | copy-start | bytes 30724
  6.1 38.8 %all-to-all-start = ((bf16[8,64,2560]{2,1,0:T(8,128)(2,1)}), bf16[8,64,2560]{2,1,0:T(8,128)(2,1)}, u32[]{:S(2)}, u32[]{:S(2)}) async-start(bf16[8,64,2560]{2,1,0:T(8,128)(2,1)} %bitcast.2), calls=%async_computation | async-start | bytes 5242880 | tf_op jit(solution)/shard_map/all_to_all | solution.py:238
  44.9 4.8 %copy-start.18 = (s32[128]{0:T(128)S(1)}, s32[128]{0:T(128)}, u32[]{:S(2)}) copy-start(s32[128]{0:T(128)} %param.25) | copy-start | bytes 1540
  44.9 64.6 %all-to-all-start.1 = ((bf16[8,64,5120]{2,1,0:T(8,128)(2,1)}), bf16[8,64,5120]{2,1,0:T(8,128)(2,1)}, u32[]{:S(2)}, u32[]{:S(2)}) async-start(bf16[8,64,5120]{2,1,0:T(8,128)(2,1)} %bitcast.74), calls=%async_computation.1 | async-start | bytes 10485760 | tf_op jit(solution)/shard_map/all_to_all | solution.py:238
  109.4 35.4 %all-to-all-start.2 = ((bf16[8,64,2560]{2,1,0:T(8,128)(2,1)}), bf16[8,64,2560]{2,1,0:T(8,128)(2,1)S(1)}, u32[]{:S(2)}, u32[]{:S(2)}) async-start(bf16[8,64,2560]{2,1,0:T(8,128)(2,1)} %bitcast.76), calls=%async_computation.2 | async-start | bytes 5242880 | tf_op jit(solution)/shard_map/all_to_all | solution.py:238
  113.3 5.3 %copy-start.21 = (bf16[1,1,2560,768]{3,2,1,0:T(8,128)(2,1)S(1)}, bf16[1,1,2560,768]{3,2,1,0:T(8,128)(2,1)}, u32[]{:S(2)}) copy-start(bf16[1,1,2560,768]{3,2,1,0:T(8,128)(2,1)} %param.21) | copy-start | bytes 11796484
  118.5 4.6 %copy-start.23 = (f32[512,768]{1,0:T(8,128)}, f32[512,768]{1,0:T(8,128)S(1)}, u32[]{:S(2)}) copy-start(f32[512,768]{1,0:T(8,128)S(1)} %fusion.10) | copy-start | bytes 4718596
  118.5 4.6 %copy-start.19 = (bf16[1,1,768,2560]{3,2,1,0:T(8,128)(2,1)S(1)}, bf16[1,1,768,2560]{3,2,1,0:T(8,128)(2,1)}, u32[]{:S(2)}) copy-start(bf16[1,1,768,2560]{3,2,1,0:T(8,128)(2,1)} %param.22) | copy-start | bytes 11796484
  123.1 5.0 %copy-start.25 = (f32[512,768]{1,0:T(8,128)}, f32[512,768]{1,0:T(8,128)S(1)}, u32[]{:S(2)}) copy-start(f32[512,768]{1,0:T(8,128)S(1)} %fusion.4) | copy-start | bytes 4718596
  123.1 5.0 %copy-start.20 = (bf16[1,1,2560,768]{3,2,1,0:T(8,128)(2,1)S(1)}, bf16[1,1,2560,768]{3,2,1,0:T(8,128)(2,1)}, u32[]{:S(2)}) copy-start(bf16[1,1,2560,768]{3,2,1,0:T(8,128)(2,1)} %param.20) | copy-start | bytes 11796484
  128.1 2.3 copy-start.22
  128.1 2.3 copy-start.27
  144.9 1.5 copy-start.2
  146.4 62.4 %all-to-all-start.3 = ((bf16[8,64,2560]{2,1,0:T(8,128)(2,1)}), bf16[8,64,2560]{2,1,0:T(8,128)(2,1)S(1)}, u32[]{:S(2)}, u32[]{:S(2)}) async-start(bf16[8,64,2560]{2,1,0:T(8,128)(2,1)} %bitcast.75), calls=%async_computation.3 | async-start | bytes 5242880 | tf_op jit(solution)/shard_map/all_to_all | solution.py:238
  150.0 1.7 copy-start.3
  153.3 0.6 copy-start.11
  153.9 0.8 copy-start.13
  154.8 26.2 %collective-permute-start.1 = (f32[8,512]{1,0:T(8,128)S(1)}, f32[8,512]{1,0:T(8,128)S(1)}, u32[]{:S(2)}, u32[]{:S(2)}) collective-permute-start(f32[8,512]{1,0:T(8,128)S(1)} %broadcast_select_fusion), channel_id=1, source_target_pairs={{0,1},{1,0},{2,3},{3,2},{4,5},{5,4},{6,7},{7,6},{8,9},{9,8},{10,11... | collective-permute-start | bytes 49160 | tf_op jit(solution)/shard_map/ppermute | solution.py:306
  181.1 3.7 %collective-permute-start.2 = (f32[8,512]{1,0:T(8,128)S(1)}, f32[8,512]{1,0:T(8,128)S(1)}, u32[]{:S(2)}, u32[]{:S(2)}) collective-permute-start(f32[8,512]{1,0:T(8,128)S(1)} %fusion.29), channel_id=1, source_target_pairs={{0,2},{1,3},{2,0},{3,1},{4,6},{5,7},{6,4},{7,5},{8,10},{9,11},{10,... | collective-permute-start | bytes 49160 | tf_op jit(solution)/shard_map/ppermute | solution.py:306
  184.9 5.3 %collective-permute-start.3 = (f32[8,512]{1,0:T(8,128)S(1)}, f32[8,512]{1,0:T(8,128)S(1)}, u32[]{:S(2)}, u32[]{:S(2)}) collective-permute-start(f32[8,512]{1,0:T(8,128)S(1)} %fusion.36), channel_id=1, source_target_pairs={{0,4},{1,5},{2,6},{3,7},{4,0},{5,1},{6,2},{7,3},{8,12},{9,13},{10,... | collective-permute-start | bytes 49160 | tf_op jit(solution)/shard_map/ppermute | solution.py:306
  187.6 21.2 %collective-permute-start = (bf16[128,2560]{1,0:T(8,128)(2,1)}, bf16[128,2560]{1,0:T(8,128)(2,1)}, u32[]{:S(2)}, u32[]{:S(2)}) collective-permute-start(bf16[128,2560]{1,0:T(8,128)(2,1)} %copy-done.13), channel_id=1, source_target_pairs={{0,8},{8,16},{16,24},{24,32},{32,40},{40,48},{48,56},{56,64},{64,7... | collective-permute-start | bytes 1966088 | tf_op jit(solution)/shard_map/ppermute | solution.py:20
  190.3 6.2 %copy-start.28 = (bf16[512,768]{1,0:T(8,128)(2,1)S(1)}, bf16[512,768]{1,0:T(8,128)(2,1)}, u32[]{:S(2)}) copy-start(bf16[512,768]{1,0:T(8,128)(2,1)} %copy-done.27) | copy-start | bytes 2359300
  196.5 6.1 %copy-start.24 = (f32[512,768]{1,0:T(8,128)S(1)}, f32[512,768]{1,0:T(8,128)}, u32[]{:S(2)}) copy-start(f32[512,768]{1,0:T(8,128)} %copy-done.23) | copy-start | bytes 4718596
  196.5 6.1 %copy-start.26 = (f32[512,768]{1,0:T(8,128)S(1)}, f32[512,768]{1,0:T(8,128)}, u32[]{:S(2)}) copy-start(f32[512,768]{1,0:T(8,128)} %copy-done.25) | copy-start | bytes 4718596
  202.7 6.1 %copy-start.10 = (f32[1,2560]{1,0:T(1,128)S(1)}, f32[1,2560]{1,0:T(1,128)}, u32[]{:S(2)}) copy-start(f32[1,2560]{1,0:T(1,128)} %refs_6_.1) | copy-start | bytes 30724
  202.7 6.1 %copy-start.12 = (f32[128,1]{1,0:T(8,128)S(1)}, f32[128,1]{1,0:T(8,128)}, u32[]{:S(2)}) copy-start(f32[128,1]{1,0:T(8,128)} %copy-done.11) | copy-start | bytes 1540
  208.8 1.1 copy-start.5
  209.9 1.1 copy-start.7
  213.4 18.0 %collective-permute-start.4 = (bf16[128,2560]{1,0:T(8,128)(2,1)}, bf16[128,2560]{1,0:T(8,128)(2,1)S(1)}, u32[]{:S(2)}, u32[]{:S(2)}) collective-permute-start(bf16[128,2560]{1,0:T(8,128)(2,1)} %get-tuple-element.33), channel_id=1, source_target_pairs={{8,0},{16,8},{24,16},{32,24},{40,32},{48,40},{56,48},{64,56},{72,6... | collective-permute-start | bytes 1966088 | tf_op jit(solution)/shard_map/ppermute | solution.py:20
  221.0 9.7 %all-to-all-start.4 = ((f32[8,1,2560]{2,1,0:T(1,128)}), f32[8,1,2560]{2,1,0:T(1,128)S(1)}, u32[]{:S(2)}, u32[]{:S(2)}) async-start(f32[8,1,2560]{2,1,0:T(1,128)} %broadcast_in_dim.68), calls=%async_computation.4 | async-start | bytes 163840 | tf_op jit(solution)/shard_map/all_to_all | solution.py:332

commit v2 on v0

--- a/solution.py
+++ b/solution.py
@@ -10,6 +10,7 @@
 bf16 = jnp.bfloat16
 f32 = jnp.float32
 chunk = 512
+extra = 128
 vmem = pl.BlockSpec(memory_space=pltpu.VMEM)
 smem = pl.BlockSpec(memory_space=pltpu.SMEM)
 
@@ -85,6 +86,7 @@
     back_gates_ref,
     rows_ref,
     dout_ref,
+    x_ref,
 ):
     is_last = last_ref[0] == 1
     ids = jnp.where(is_last, fwd_ids_ref[...], back_ids_ref[...])
@@ -93,7 +95,9 @@
     pick = (hit0 | hit1).astype(bf16)
     high, low = split_weights(hit0, hit1, gates)
     x = jnp.where(is_last, fwd_ref[...].astype(f32), back_ref[...].astype(f32))
+    x_ref[...] = x.astype(bf16)
     normed = (x * inv_rms_of(x) * gain_ref[...]).astype(bf16)
+    dout_ref[:, x.shape[1] :] = jnp.zeros((dout_ref.shape[0], extra), bf16)
     for cols in chunks(x.shape[1]):
         rows_ref[:, cols] = over_tokens(pick, normed[:, cols]).astype(bf16)
         cot = cot_ref[:, cols]
@@ -107,46 +111,81 @@
         ).astype(bf16)
 
 
-def join_forward(
+def in_parts(column):
+    lanes = lax.broadcasted_iota(jnp.int32, (column.shape[0], extra), 1)
+    out = jnp.zeros((column.shape[0], extra), f32)
+    rest = column
+    for lane in range(3):
+        part = rest.astype(bf16).astype(f32)
+        out = jnp.where(lanes == lane, part, out)
+        rest = rest - part
+    return out.astype(bf16)
+
+
+def attach_dots(out_ref, head_ref, unused_ref, block_ref, ret_ref):
+    width = out_ref.shape[1]
+    dots = jnp.zeros((out_ref.shape[0], 1), f32)
+    for cols in chunks(width):
+        out = out_ref[:, cols]
+        ret_ref[:, cols] = out
+        dots += jnp.sum(out.astype(f32) * head_ref[:, cols], axis=1, keepdims=True)
+    ret_ref[:, width:] = jnp.zeros((out_ref.shape[0], extra), bf16)
+    block_ref[...] = in_parts(dots)
+
+
+def find_coefs(
+    groups,
+    capacity,
+    last_ref,
+    x_ref,
+    ids_ref,
+    gates_ref,
+    head_ref,
+    labels_ref,
+    dots_ref,
+    unused_ref,
+    coef_ref,
+    block_ref,
+):
+    is_last = last_ref[0] == 1
+    hit0, hit1 = slot_hits(ids_ref[...], groups, capacity)
+    high, low = split_weights(hit0, hit1, gates_ref[...])
+    pick = (hit0 | hit1).astype(bf16)
+    dots = dots_ref[...]
+    mixed = jnp.dot(high, dots, preferred_element_type=f32) + jnp.dot(
+        low, dots, preferred_element_type=f32
+    )
+    logits = jnp.sum(mixed, axis=1, keepdims=True)
+    logits += jnp.sum(x_ref[...].astype(f32) * head_ref[...], axis=1, keepdims=True)
+    coef = loss_scale * (jax.nn.sigmoid(logits) - labels_ref[...].astype(f32))
+    coef = jnp.where(is_last, coef, 1.0)
+    coef_ref[...] = coef
+    picked = over_tokens(pick, in_parts(coef))
+    ones = (lax.broadcasted_iota(jnp.int32, picked.shape, 1) == 0).astype(f32)
+    block_ref[...] = jnp.where(is_last, picked, ones).astype(bf16)
+
+
+def join_forward(groups, capacity, ret_ref, x_ref, ids_ref, gates_ref, out_ref):
+    hit0, hit1 = slot_hits(ids_ref[...], groups, capacity)
+    high, low = split_weights(hit0, hit1, gates_ref[...])
+    for cols in chunks(x_ref.shape[1]):
+        ret = ret_ref[:, cols]
+        mixed = jnp.dot(high, ret, preferred_element_type=f32) + jnp.dot(
+            low, ret, preferred_element_type=f32
+        )
+        out_ref[:, cols] = (x_ref[:, cols].astype(f32) + mixed).astype(bf16)
+
+
+def copy_rows(in_ref, out_ref):
+    out_ref[...] = in_ref[...]
+
+
+def join_backward(
     groups,
     capacity,
     last_ref,
     ret_ref,
     x_ref,
-    ids_ref,
-    gates_ref,
-    head_ref,
-    labels_ref,
-    out_ref,
-    coef_ref,
-    slots_ref,
-):
-    is_last = last_ref[0] == 1
-    hit0, hit1 = slot_hits(ids_ref[...], groups, capacity)
-    high, low = split_weights(hit0, hit1, gates_ref[...])
-    logits = jnp.zeros((x_ref.shape[0], 1), f32)
-    for cols in chunks(x_ref.shape[1]):
-        ret = ret_ref[:, cols]
-        mixed = jnp.dot(high, ret, preferred_element_type=f32) + jnp.dot(
-            low, ret, preferred_element_type=f32
-        )
-        out = (x_ref[:, cols].astype(f32) + mixed).astype(bf16)
-        out_ref[:, cols] = out
-        logits += jnp.sum(out.astype(f32) * head_ref[:, cols], axis=1, keepdims=True)
-    coef = loss_scale * (jax.nn.sigmoid(logits) - labels_ref[...].astype(f32))
-    coef = jnp.where(is_last, coef, 1.0)
-    coef_ref[...] = coef
-    picked = jnp.sum(jnp.where(hit0 | hit1, coef, 0.0), axis=0, keepdims=True)
-    slots_ref[...] = jnp.where(is_last, picked, 1.0)
-
-
-def join_backward(
-    groups,
-    capacity,
-    last_ref,
-    ret_ref,
-    fwd_ref,
-    back_ref,
     cot_ref,
     coef_ref,
     gain_ref,
@@ -162,7 +201,7 @@
     hit0, hit1 = slot_hits(ids, groups, capacity)
     pick = (hit0 | hit1).astype(bf16)
     coef = coef_ref[...]
-    x = jnp.where(is_last, fwd_ref[...].astype(f32), back_ref[...].astype(f32))
+    x = x_ref[...].astype(f32)
     inv = inv_rms_of(x)
     dots = jnp.zeros((x.shape[0], 1), f32)
     for cols in chunks(x.shape[1]):
@@ -179,13 +218,15 @@
         ).astype(bf16)
 
 
-def call(kernel, name, outs, args, specs, scratch=()):
+def call(kernel, name, outs, args, specs, scratch=(), out_specs=None, aliases=None):
     return pl.pallas_call(
         kernel,
         out_shape=[jax.ShapeDtypeStruct(shape, dtype) for shape, dtype in outs],
+        grid=(1,),
         in_specs=specs,
-        out_specs=[vmem] * len(outs),
+        out_specs=out_specs or [vmem] * len(outs),
         scratch_shapes=list(scratch),
+        input_output_aliases=aliases or {},
         compiler_params=pltpu.CompilerParams(vmem_limit_bytes=48 << 20),
         name=name,
     )(*args)
@@ -237,9 +278,13 @@
 
     def exchange(value):
         out = lax.all_to_all(
-            value.reshape(groups, capacity, width), "expert", split_axis=0, concat_axis=0, tiled=True
+            value.reshape(groups, capacity, value.shape[1]),
+            "expert",
+            split_axis=0,
+            concat_axis=0,
+            tiled=True,
         )
-        return out.reshape(slots, width)
+        return out.reshape(value.shape)
 
     (send_f,) = call(
         bind(send_forward),
@@ -249,10 +294,11 @@
         [vmem] * 3,
     )
     rows_f = exchange(send_f)
-    send_b, send_d = call(
+    last_block = pl.BlockSpec((slots, extra), lambda i: (0, width // extra))
+    send_b, send_d, x_sel = call(
         bind(send_backward),
         "send_backward",
-        [((slots, width), bf16)] * 2,
+        [((slots, width), bf16), ((slots, width + extra), bf16), ((tok_dev, width), bf16)],
         (
             last,
             x_fwd,
@@ -267,22 +313,49 @@
         ),
         [smem] + [vmem] * 9,
     )
-    rows_f, send_b, send_d = lax.optimization_barrier((rows_f, send_b, send_d))
+    rows_f, send_b = lax.optimization_barrier((rows_f, send_b))
     rows_b = exchange(send_b)
     gate_pre = jnp.dot(rows_f, wg, preferred_element_type=f32)
     up_pre = jnp.dot(rows_f, wu, preferred_element_type=f32)
     hidden_f = (jax.nn.silu(gate_pre) * up_pre).astype(bf16)
     out_f = jnp.dot(hidden_f, wd, preferred_element_type=f32).astype(bf16)
+    send_d, ret_send = call(
+        attach_dots,
+        "attach_dots",
+        [((slots, width + extra), bf16)] * 2,
+        (out_f, head, send_d),
+        [vmem, vmem, last_block],
+        out_specs=[last_block, vmem],
+        aliases={2: 0},
+    )
     rows_b, send_d = lax.optimization_barrier((rows_b, send_d))
     rows_d = exchange(send_d)
-    rows_d, out_f = lax.optimization_barrier((rows_d, out_f))
-    ret_f = exchange(out_f)
+    coef, ret_send = call(
+        bind(find_coefs),
+        "find_coefs",
+        [((tok_dev, 1), f32), ((slots, width + extra), bf16)],
+        (
+            last,
+            x_fwd,
+            fwd_routes[0],
+            fwd_gates[0],
+            head,
+            verdict_labels[:, None],
+            rows_d,
+            ret_send,
+        ),
+        [smem] + [vmem] * 5 + [last_block] * 2,
+        out_specs=[vmem, last_block],
+        aliases={7: 1},
+    )
+    ret_f = exchange(ret_send)
 
     gate_pre = jnp.dot(rows_b, wg, preferred_element_type=f32)
     up_pre = jnp.dot(rows_b, wu, preferred_element_type=f32)
     sig = jax.nn.sigmoid(gate_pre)
     silu = gate_pre * sig
     hidden_b = (silu * up_pre).astype(bf16)
+    rows_d = rows_d[:, :width]
     d_hidden = contract_cols(rows_d, wd)
     d_gate = (d_hidden * up_pre * sig * (1.0 + gate_pre * (1.0 - sig))).astype(bf16)
     d_up = (d_hidden * silu).astype(bf16)
@@ -290,17 +363,18 @@
 
     ret_f, d_rows = lax.optimization_barrier((ret_f, d_rows))
     ret_d = exchange(d_rows)
-    layer_out, coef, coef_slots = call(
+    (layer_out,) = call(
         bind(join_forward),
         "join_forward",
-        [((tok_dev, width), bf16), ((tok_dev, 1), f32), ((1, slots), f32)],
-        (last, ret_f, x_fwd, fwd_routes[0], fwd_gates[0], head, verdict_labels[:, None]),
-        [smem] + [vmem] * 6,
+        [((tok_dev, width), bf16)],
+        (ret_f, x_fwd, fwd_routes[0], fwd_gates[0]),
+        [vmem] * 4,
     )
     next_input = passed_along(layer_out, "section", 1)
-    coef_rows = lax.all_to_all(
-        coef_slots.reshape(groups, 1, capacity), "expert", split_axis=0, concat_axis=0, tiled=True
-    ).reshape(slots, 1)
+    (next_input,) = call(
+        copy_rows, "copy_rows", [((tok_dev, width), bf16)], (next_input,), [vmem]
+    )
+    coef_rows = jnp.sum(ret_f[:, width:].astype(f32), axis=1, keepdims=True)
 
     def scaled(value):
         return (value.astype(f32) * coef_rows).astype(bf16)
@@ -309,12 +383,15 @@
     grad_g = contract_rows(rows_b, scaled(d_gate)).astype(bf16)
     grad_u = contract_rows(rows_b, scaled(d_up)).astype(bf16)
 
+    ret_d, next_input, grad_d, grad_g, grad_u = lax.optimization_barrier(
+        (ret_d, next_input, grad_d, grad_g, grad_u)
+    )
     d_input, gain_local = call(
         bind(join_backward),
         "join_backward",
         [((tok_dev, width), bf16), ((1, width), f32)],
-        (last, ret_d, x_fwd, x_back, cot, coef, norm_gain, head, fwd_routes[0], back_routes[0]),
-        [smem] + [vmem] * 9,
+        (last, ret_d, x_sel, cot, coef, norm_gain, head, fwd_routes[0], back_routes[0]),
+        [smem] + [vmem] * 8,
         [pltpu.VMEM((tok_dev, width), f32)],
     )
     prev_grad = passed_along(d_input, "section", -1)

time: 229 us -> 224 us (0.978)
  waiting for transfers between devices: 104 us -> 94.4 us
  Pallas kernels: 12.1 us -> 18.2 us
  blocking collectives: 8.68 us -> 14.3 us
  starting transfers between devices: 32.1 us -> 27.3 us
    all_to_all x6 -> x5, waiting for transfers between devices: 104 us -> 78.8 us  [exchange(): lax.all_to_all(value.reshape(groups, capacity, value.shape[1]), 'expert',...]
    ppermute x2, waiting for transfers between devices: 0.01 us -> 15.6 us  [passed_along(): lax.ppermute(value, axis, [(source, source + steps) for source in range(i...]
    pallas_call x4 -> x7, Pallas kernels: 12.1 us -> 18.2 us  [call(): pl.pallas_call(kernel, out_shape=[jax.ShapeDtypeStruct(shape, dtype) for...]
    all_to_all x1, blocking collectives: 8.68 us -> 14.3 us  [on_device(): lax.all_to_all(jnp.broadcast_to(gain_local[None], (groups, 1, width)), 'e...]
    all_to_all x6 -> x5, starting transfers between devices: 27.4 us -> 23.3 us  [exchange(): lax.all_to_all(value.reshape(groups, capacity, value.shape[1]), 'expert',...]
    unnamed x62 -> x73, local copies, waits for them, and re-layouts: 9.85 us -> 9.6 us
  transfers between devices with their start and end apart: 8 -> 7, of which waited for: 6 -> 5; matrix products, arithmetic and copies ran while one was open for 26% -> 26% of each run, Pallas kernels for 3% -> 5%
where the time goes in v2:
time: 224 us
  waiting for transfers between devices  94.4 us (42%)
  matrix products  57.2 us (26%)
  starting transfers between devices  27.3 us (12%)
  Pallas kernels  18.2 us (8%)
  blocking collectives  14.3 us (6%)
  local copies, waits for them, and re-layouts  11 us (5%)
    all_to_all x5, waiting for transfers between devices, exchange(): lax.all_to_all(value.reshape(groups, capacity, value.shape[1]), 'expert',...  78.8 us
    all_to_all x5, starting transfers between devices, exchange(): lax.all_to_all(value.reshape(groups, capacity, value.shape[1]), 'expert',...  23.3 us
    dot_general x3, matrix products, contract_rows(): lax.dot_general(left_op, right_op, (((0,), (0,)), ((), ())), preferred_el...  18.3 us
    pallas_call x7, Pallas kernels, call(): pl.pallas_call(kernel, out_shape=[jax.ShapeDtypeStruct(shape, dtype) for...  18.2 us
    ppermute x2, waiting for transfers between devices, passed_along(): lax.ppermute(value, axis, [(source, source + steps) for source in range(i...  15.6 us
    all_to_all x1, blocking collectives, on_device(): lax.all_to_all(jnp.broadcast_to(gain_local[None], (groups, 1, width)), 'e...  14.3 us
    dot_general x3, matrix products, contract_cols(): lax.dot_general(left_op, right_op, (((1,), (1,)), ((), ())), preferred_el...  11 us
    dot_general x1, matrix products, on_device(): out_f = jnp.dot(hidden_f, wd, preferred_element_type=f32).astype(bf16)  10.1 us
  transfers between devices with their start and end apart: 7, of which 5 were waited for; matrix products, arithmetic and copies ran while one was open for 26% of the time, Pallas kernels for 5%

profile of v2, /device:TPU:4, one launch (start us, length us, event | category | flops | bytes accessed | tf_op | source)
XLA Modules:
  0.0 223.7 jit_solution(11653467384440714195)
XLA Ops:
  0.6 0.8 copy.31
  1.4 1.1 copy-done.2
  2.5 0.7 copy-done.13
  3.2 2.8 %send_forward.1 = bf16[512,2560]{1,0:T(8,128)(2,1)} custom-call(bf16[128,2560]{1,0:T(8,128)(2,1)S(1)} %bitcast.60, f32[1,2560]{1,0:T(1,128)S(1)} %copy-done.13, s32[128,2]{1,0:T(8,128)S(1)} %bitcast.67), custom_call_target="tpu_custom_call" | custom-call | tf_op jit(solution)/shard_map/send_forward/pallas_call | solution.py:222
  6.0 0.0 copy-start.3
  6.0 0.0 copy-start.4
  6.0 0.0 copy-start.7
  6.1 0.0 copy-start.14
  6.1 6.1 %all-to-all-start = ((bf16[8,64,2560]{2,1,0:T(8,128)(2,1)}), bf16[8,64,2560]{2,1,0:T(8,128)(2,1)}, u32[]{:S(2)}, u32[]{:S(2)}) async-start(bf16[8,64,2560]{2,1,0:T(8,128)(2,1)} %bitcast.5), calls=%async_computation | async-start | bytes 5242880 | tf_op jit(solution)/shard_map/all_to_all | solution.py:280
  12.2 0.1 copy.33
  12.3 0.0 copy-done.20
  12.3 0.1 copy.32
  12.4 0.1 copy.34
  12.6 0.0 copy-done.4
  12.6 0.0 copy-done.7
  12.6 0.0 copy-done.14
  12.6 5.0 %send_backward.1 = (bf16[512,2560]{1,0:T(8,128)(2,1)S(1)}, bf16[512,2688]{1,0:T(8,128)(2,1)}, bf16[128,2560]{1,0:T(8,128)(2,1)S(1)}) custom-call(s32[1]{0:T(128)} %bitcast.refs_0_, bf16[128,2560]{1,0:T(8,128)(2,1)S(1)} %bitcast.61, bf16[128,2560]{1,0:T(8,128)(2,1)S(1)} %bitcast.75, bf16[128,2560]{1,0:T(8,128)(2,1)S(1)} %bitcast.64, ...), custom_call_target="tpu_custom_call" | custom-call | tf_op jit(solution)/shard_map/send_backward/pallas_call | solution.py:222
  17.6 1.5 copy-done.6
  19.1 0.8 copy-done.8
  19.9 24.9 %all-to-all-done = bf16[8,64,2560]{2,1,0:T(8,128)(2,1)} async-done(((bf16[8,64,2560]{2,1,0:T(8,128)(2,1)}), bf16[8,64,2560]{2,1,0:T(8,128)(2,1)}, u32[]{:S(2)}, u32[]{:S(2)}) %all-to-all-start) | async-done | bytes 2621472 | tf_op jit(solution)/shard_map/all_to_all | solution.py:280
  44.9 4.4 %all-to-all-start.1 = ((bf16[8,64,2560]{2,1,0:T(8,128)(2,1)}), bf16[8,64,2560]{2,1,0:T(8,128)(2,1)}, u32[]{:S(2)}, u32[]{:S(2)}) async-start(bf16[8,64,2560]{2,1,0:T(8,128)(2,1)} %bitcast.66), calls=%async_computation.1 | async-start | bytes 5242880 | tf_op jit(solution)/shard_map/all_to_all | solution.py:280
  49.3 6.2 %fusion.12 = f32[512,768]{1,0:T(8,128)} fusion(bf16[512,2560]{1,0:T(8,128)(2,1)} %bitcast.6, bf16[1,1,2560,768]{3,2,1,0:T(8,128)(2,1)} %param.20), kind=kOutput, calls=%fused_computation.17 | convolution fusion | flops 2013265920 | bytes 8126464 | tf_op jit(solution)/shard_map/dot_general | solution.py:318
  55.5 10.1 %convolution_convert_fusion.3.out_ref = bf16[512,2560]{1,0:T(8,128)(2,1)S(1)} fusion(bf16[1,1,768,2560]{3,2,1,0:T(8,128)(2,1)} %param.22, f32[512,768]{1,0:T(8,128)} %fusion.12, bf16[512,2560]{1,0:T(8,128)(2,1)} %bitcast.6, bf16[1,1,2560,768]{3,2,1,0:T(8,128)(2,1)} %param.21), kind=kOutput, calls=%fused_computation.4 | convolution fusion | flops 4030201856 | bytes 14680064 | tf_op jit(solution)/shard_map/dot_general | solution.py:321
  65.6 3.1 %attach_dots.1 = (bf16[512,2688]{1,0:T(8,128)(2,1)}, bf16[512,2688]{1,0:T(8,128)(2,1)}) custom-call(bf16[512,2560]{1,0:T(8,128)(2,1)S(1)} %convolution_convert_fusion.3.out_ref, f32[1,2560]{1,0:T(1,128)S(1)} %broadcast_in_dim.37.refs_5_.head_ref.refs_4_.refs_6_, bf16[512,2688]{1,0:T(8,128)(2,1)} %get-tuple-element.29.unused_ref), custom_call_target="tpu_custom_call", output_to_operand_aliasing={{0}: (2, {})} | custom-call | tf_op jit(solution)/shard_map/attach_dots/pallas_call | solution.py:222
  68.7 12.3 %all-to-all-done.1 = bf16[8,64,2560]{2,1,0:T(8,128)(2,1)} async-done(((bf16[8,64,2560]{2,1,0:T(8,128)(2,1)}), bf16[8,64,2560]{2,1,0:T(8,128)(2,1)}, u32[]{:S(2)}, u32[]{:S(2)}) %all-to-all-start.1) | async-done | bytes 2621472 | tf_op jit(solution)/shard_map/all_to_all | solution.py:280
  81.0 4.7 %all-to-all-start.2 = ((bf16[8,64,2688]{2,1,0:T(8,128)(2,1)}), bf16[8,64,2688]{2,1,0:T(8,128)(2,1)}, u32[]{:S(2)}, u32[]{:S(2)}) async-start(bf16[8,64,2688]{2,1,0:T(8,128)(2,1)} %bitcast.16), calls=%async_computation.2 | async-start | bytes 5505024 | tf_op jit(solution)/shard_map/all_to_all | solution.py:280
  85.7 0.7 copy.35.refs_5_
  86.5 6.4 %fusion.10 = f32[512,768]{1,0:T(8,128)} fusion(bf16[512,2560]{1,0:T(8,128)(2,1)} %bitcast.12, bf16[1,1,2560,768]{3,2,1,0:T(8,128)(2,1)} %param.20), kind=kOutput, calls=%fused_computation.15 | convolution fusion | flops 2013265920 | bytes 8126464 | tf_op jit(solution)/shard_map/dot_general | solution.py:353
  92.9 25.2 %all-to-all-done.2 = bf16[8,64,2688]{2,1,0:T(8,128)(2,1)} async-done(((bf16[8,64,2688]{2,1,0:T(8,128)(2,1)}), bf16[8,64,2688]{2,1,0:T(8,128)(2,1)}, u32[]{:S(2)}, u32[]{:S(2)}) %all-to-all-start.2) | async-done | bytes 2752544 | tf_op jit(solution)/shard_map/all_to_all | solution.py:280
  118.1 0.8 copy-done.12
  118.9 1.9 find_coefs.1
  120.8 0.0 copy-start.1
  120.9 1.5 copy-done.1
  122.4 0.6 copy-done.16
  123.0 3.6 %all-to-all-start.3 = ((bf16[8,64,2688]{2,1,0:T(8,128)(2,1)}), bf16[8,64,2688]{2,1,0:T(8,128)(2,1)S(1)}, u32[]{:S(2)}, u32[]{:S(2)}) async-start(bf16[8,64,2688]{2,1,0:T(8,128)(2,1)} %bitcast.59), calls=%async_computation.3 | async-start | bytes 5505024 | tf_op jit(solution)/shard_map/all_to_all | solution.py:280
  126.6 0.0 copy-start.23
  126.7 5.2 %fusion.4 = f32[512,768]{1,0:T(8,128)S(1)} fusion(bf16[512,2560]{1,0:T(8,128)(2,1)} %bitcast.12, bf16[1,1,2560,768]{3,2,1,0:T(8,128)(2,1)} %param.21), kind=kOutput, calls=%fused_computation.9 | convolution fusion | flops 2013265920 | bytes 8126464 | tf_op jit(solution)/shard_map/dot_general | solution.py:354
  131.9 0.0 copy-start.24
  132.0 4.9 %multiply_convert_fusion.4 = (bf16[512,768]{1,0:T(8,128)(2,1)S(1)}, bf16[512,768]{1,0:T(8,128)(2,1)S(1)}) fusion(f32[512,768]{1,0:T(8,128)S(1)} %copy-done.30, f32[512,768]{1,0:T(8,128)S(1)} %fusion.4, bf16[1,1,768,2560]{3,2,1,0:T(8,128)(2,1)S(1)} %copy-done.23, bf16[512,2688]{1,0:T(8,128)(2,1)} %bitcast.17.refs_6_), kind=kOutput, calls=%fused_computation.25 | convolution fusion | flops 2018377728 | bytes 11272192 | tf_op jit(solution)/shard_map/dot_general | solution.py:242
  136.9 0.0 copy-start.26
  136.9 0.0 copy-start.25
  136.9 2.2 fusion.8
  139.2 0.4 copy-done.25
  139.6 3.8 %add_convert_fusion = bf16[512,2560]{1,0:T(8,128)(2,1)} fusion(f32[512,2560]{1,0:T(8,128)S(1)} %fusion.8, bf16[512,768]{1,0:T(8,128)(2,1)S(1)} %get-tuple-element.46, bf16[1,1,2560,768]{3,2,1,0:T(8,128)(2,1)S(1)} %copy-done.25), kind=kOutput, calls=%fused_computation | convolution fusion | flops 2015887360 | bytes 12582912 | tf_op jit(solution)/shard_map/dot_general | solution.py:242
  143.4 16.5 %all-to-all-done.3 = bf16[8,64,2688]{2,1,0:T(8,128)(2,1)S(1)} async-done(((bf16[8,64,2688]{2,1,0:T(8,128)(2,1)}), bf16[8,64,2688]{2,1,0:T(8,128)(2,1)S(1)}, u32[]{:S(2)}, u32[]{:S(2)}) %all-to-all-start.3) | async-done | bytes 2752544 | tf_op jit(solution)/shard_map/all_to_all | solution.py:280
  159.9 4.4 %all-to-all-start.4 = ((bf16[8,64,2560]{2,1,0:T(8,128)(2,1)}), bf16[8,64,2560]{2,1,0:T(8,128)(2,1)}, u32[]{:S(2)}, u32[]{:S(2)}) async-start(bf16[8,64,2560]{2,1,0:T(8,128)(2,1)} %bitcast.79), calls=%async_computation.4 | async-start | bytes 5242880 | tf_op jit(solution)/shard_map/all_to_all | solution.py:280
  164.3 0.0 copy-start.27
  164.3 1.3 join_forward.1
  165.6 2.1 collective-permute-start
  167.8 0.1 convert_reduce_fusion
  167.9 6.0 %convolution_convert_fusion.1 = bf16[2560,768]{1,0:T(8,128)(2,1)} fusion(bf16[512,2560]{1,0:T(8,128)(2,1)} %bitcast.12, bf16[512,768]{1,0:T(8,128)(2,1)S(1)} %copy-done.27, f32[512]{0:T(512)S(1)} %convert_reduce_fusion), kind=kOutput, calls=%fused_computation.2 | convolution fusion | flops 2016411648 | bytes 7342080 | tf_op jit(solution)/shard_map/dot_general | solution.py:236
  174.0 6.1 %convolution_convert_fusion = bf16[2560,768]{1,0:T(8,128)(2,1)} fusion(bf16[512,2560]{1,0:T(8,128)(2,1)} %bitcast.12, bf16[512,768]{1,0:T(8,128)(2,1)S(1)} %copy-done.29, f32[512]{0:T(512)S(1)} %convert_reduce_fusion), kind=kOutput, calls=%fused_computation.1 | convolution fusion | flops 2016411648 | bytes 7342080 | tf_op jit(solution)/shard_map/dot_general | solution.py:236
  180.1 0.0 copy-start.15
  180.1 6.1 %convolution_convert_fusion.2 = bf16[768,2560]{1,0:T(8,128)(2,1)} fusion(bf16[512,2688]{1,0:T(8,128)(2,1)} %bitcast.17.refs_6_, f32[512,768]{1,0:T(8,128)S(1)} %copy-done.33, f32[512]{0:T(512)S(1)} %convert_reduce_fusion, f32[512,768]{1,0:T(8,128)S(1)} %copy-done.31), kind=kOutput, calls=%fused_computation.3 | convolution fusion | flops 2018770944 | bytes 9701376 | tf_op jit(solution)/shard_map/dot_general | solution.py:236
  186.3 15.6 %collective-permute-done.in_ref = bf16[128,2560]{1,0:T(8,128)(2,1)S(1)} collective-permute-done((bf16[128,2560]{1,0:T(8,128)(2,1)S(1)}, bf16[128,2560]{1,0:T(8,128)(2,1)S(1)}, u32[]{:S(2)}, u32[]{:S(2)}) %collective-permute-start) | collective-permute-done | bytes 655392 | tf_op jit(solution)/shard_map/ppermute | solution.py:21
  201.8 0.9 copy_rows.1
  202.7 0.0 all-to-all-done.4
  202.7 3.1 %join_backward.1 = (bf16[128,2560]{1,0:T(8,128)(2,1)S(1)}, f32[1,2560]{1,0:T(1,128)S(1)}) custom-call(s32[1]{0:T(128)} %bitcast.refs_0_, bf16[512,2560]{1,0:T(8,128)(2,1)} %bitcast.21.refs_1_, bf16[128,2560]{1,0:T(8,128)(2,1)S(1)} %copy-done.9, bf16[128,2560]{1,0:T(8,128)(2,1)S(1)} %bitcast.65, f32[128,1]{1,0:T(8,128)S(1)} %copy-done.17, ...), custom_call_target="tpu_custom_call" | custom-call | tf_op jit(solution)/shard_map/join_backward/pallas_call | solution.py:222
  205.8 1.9 collective-permute-start.1
  207.9 14.3 %all_to_all.30 = f32[8,1,2560]{2,1,0:T(1,128)S(1)} all-to-all(f32[8,1,2560]{2,1,0:T(1,128)S(1)} %broadcast_in_dim.42), channel_id=1, replica_groups=mesh['section'=16,'expert'=8] {'expert'}, dimensions={0} | all-to-all | bytes 163840 | tf_op jit(solution)/shard_map/all_to_all | solution.py:398
  222.1 0.1 reduce_sum.21
  222.2 0.6 reduce_sum.22
  222.8 0.0 collective-permute-done.1
  222.8 0.8 copy.41
  (48 shorter events, 0.2 us)
Async XLA Ops:
  1.4 1.1 copy-start.2
  2.5 0.7 copy-start.13
  6.0 6.2 %copy-start.18 = (f32[2560]{0:T(1024)S(1)}, f32[2560]{0:T(1024)}, u32[]{:S(2)}) copy-start(f32[2560]{0:T(1024)} %param.24) | copy-start | bytes 30724
  6.0 6.2 %copy-start.19 = (s32[1,128,2]{1,2,0:T(2,128)S(1)}, s32[1,128,2]{1,2,0:T(2,128)}, u32[]{:S(2)}) copy-start(s32[1,128,2]{1,2,0:T(2,128)} %param.17) | copy-start | bytes 3076
  6.0 6.3 %copy-start.20 = (f32[1,128,2]{1,2,0:T(2,128)S(1)}, f32[1,128,2]{1,2,0:T(2,128)}, u32[]{:S(2)}) copy-start(f32[1,128,2]{1,2,0:T(2,128)} %param.18) | copy-start | bytes 3076
  6.0 6.4 %copy-start.21 = (f32[1,128,2]{1,2,0:T(2,128)S(1)}, f32[1,128,2]{1,2,0:T(2,128)}, u32[]{:S(2)}) copy-start(f32[1,128,2]{1,2,0:T(2,128)} %param.19) | copy-start | bytes 3076
  6.0 6.5 %copy-start.3 = (bf16[1,128,2560]{2,1,0:T(8,128)(2,1)S(1)}, bf16[1,128,2560]{2,1,0:T(8,128)(2,1)}, u32[]{:S(2)}) copy-start(bf16[1,128,2560]{2,1,0:T(8,128)(2,1)} %param.13) | copy-start | bytes 1966084
  6.0 6.5 %copy-start.4 = (bf16[1,128,2560]{2,1,0:T(8,128)(2,1)S(1)}, bf16[1,128,2560]{2,1,0:T(8,128)(2,1)}, u32[]{:S(2)}) copy-start(bf16[1,128,2560]{2,1,0:T(8,128)(2,1)} %param.15) | copy-start | bytes 1966084
  6.0 6.5 %copy-start.7 = (bf16[1,128,2560]{2,1,0:T(8,128)(2,1)S(1)}, bf16[1,128,2560]{2,1,0:T(8,128)(2,1)}, u32[]{:S(2)}) copy-start(bf16[1,128,2560]{2,1,0:T(8,128)(2,1)} %param.14) | copy-start | bytes 1966084
  6.1 6.5 %copy-start.14 = (f32[1,2560]{1,0:T(1,128)S(1)}, f32[1,2560]{1,0:T(1,128)}, u32[]{:S(2)}) copy-start(f32[1,2560]{1,0:T(1,128)} %refs_5_.1) | copy-start | bytes 30724
  6.1 38.8 %all-to-all-start = ((bf16[8,64,2560]{2,1,0:T(8,128)(2,1)}), bf16[8,64,2560]{2,1,0:T(8,128)(2,1)}, u32[]{:S(2)}, u32[]{:S(2)}) async-start(bf16[8,64,2560]{2,1,0:T(8,128)(2,1)} %bitcast.5), calls=%async_computation | async-start | bytes 5242880 | tf_op jit(solution)/shard_map/all_to_all | solution.py:280
  12.3 32.6 %copy-start.10 = (s32[1,128,2]{2,1,0:T(8,128)}, s32[1,128,2]{2,1,0:T(8,128)S(1)}, u32[]{:S(2)}) copy-start(s32[1,128,2]{2,1,0:T(8,128)S(1)} %copy.33) | copy-start | bytes 3076
  17.6 1.5 copy-start.6
  19.1 0.8 copy-start.8
  44.9 36.1 %all-to-all-start.1 = ((bf16[8,64,2560]{2,1,0:T(8,128)(2,1)}), bf16[8,64,2560]{2,1,0:T(8,128)(2,1)}, u32[]{:S(2)}, u32[]{:S(2)}) async-start(bf16[8,64,2560]{2,1,0:T(8,128)(2,1)} %bitcast.66), calls=%async_computation.1 | async-start | bytes 5242880 | tf_op jit(solution)/shard_map/all_to_all | solution.py:280
  81.0 4.7 %copy-start.22 = (s32[128]{0:T(128)S(1)}, s32[128]{0:T(128)}, u32[]{:S(2)}) copy-start(s32[128]{0:T(128)} %param.25) | copy-start | bytes 1540
  81.0 37.1 %all-to-all-start.2 = ((bf16[8,64,2688]{2,1,0:T(8,128)(2,1)}), bf16[8,64,2688]{2,1,0:T(8,128)(2,1)}, u32[]{:S(2)}, u32[]{:S(2)}) async-start(bf16[8,64,2688]{2,1,0:T(8,128)(2,1)} %bitcast.16), calls=%async_computation.2 | async-start | bytes 5505024 | tf_op jit(solution)/shard_map/all_to_all | solution.py:280
  86.5 31.6 %copy-start = (bf16[512,2688]{1,0:T(8,128)(2,1)S(1)}, bf16[512,2688]{1,0:T(8,128)(2,1)}, u32[]{:S(2)}) copy-start(bf16[512,2688]{1,0:T(8,128)(2,1)} %get-tuple-element.32.refs_7_) | copy-start | bytes 8257540
  118.1 0.8 copy-start.12
  120.8 1.5 copy-start.1
  122.4 0.6 copy-start.16
  123.0 36.9 %all-to-all-start.3 = ((bf16[8,64,2688]{2,1,0:T(8,128)(2,1)}), bf16[8,64,2688]{2,1,0:T(8,128)(2,1)S(1)}, u32[]{:S(2)}, u32[]{:S(2)}) async-start(bf16[8,64,2688]{2,1,0:T(8,128)(2,1)} %bitcast.59), calls=%async_computation.3 | async-start | bytes 5505024 | tf_op jit(solution)/shard_map/all_to_all | solution.py:280
  126.6 5.3 %copy-start.23 = (bf16[1,1,768,2560]{3,2,1,0:T(8,128)(2,1)S(1)}, bf16[1,1,768,2560]{3,2,1,0:T(8,128)(2,1)}, u32[]{:S(2)}) copy-start(bf16[1,1,768,2560]{3,2,1,0:T(8,128)(2,1)} %param.22) | copy-start | bytes 11796484
  126.7 5.3 %copy-start.30 = (f32[512,768]{1,0:T(8,128)S(1)}, f32[512,768]{1,0:T(8,128)}, u32[]{:S(2)}) copy-start(f32[512,768]{1,0:T(8,128)} %fusion.10) | copy-start | bytes 4718596
  131.9 4.9 %copy-start.32 = (f32[512,768]{1,0:T(8,128)}, f32[512,768]{1,0:T(8,128)S(1)}, u32[]{:S(2)}) copy-start(f32[512,768]{1,0:T(8,128)S(1)} %fusion.4) | copy-start | bytes 4718596
  131.9 5.0 %copy-start.24 = (bf16[1,1,2560,768]{3,2,1,0:T(8,128)(2,1)S(1)}, bf16[1,1,2560,768]{3,2,1,0:T(8,128)(2,1)}, u32[]{:S(2)}) copy-start(bf16[1,1,2560,768]{3,2,1,0:T(8,128)(2,1)} %param.20) | copy-start | bytes 11796484
  136.9 2.3 %copy-start.26 = (bf16[512,768]{1,0:T(8,128)(2,1)}, bf16[512,768]{1,0:T(8,128)(2,1)S(1)}, u32[]{:S(2)}) copy-start(bf16[512,768]{1,0:T(8,128)(2,1)S(1)} %get-tuple-element.47) | copy-start | bytes 2359300
  136.9 2.3 %copy-start.28 = (bf16[512,768]{1,0:T(8,128)(2,1)}, bf16[512,768]{1,0:T(8,128)(2,1)S(1)}, u32[]{:S(2)}) copy-start(bf16[512,768]{1,0:T(8,128)(2,1)S(1)} %get-tuple-element.46) | copy-start | bytes 2359300
  136.9 2.7 %copy-start.25 = (bf16[1,1,2560,768]{3,2,1,0:T(8,128)(2,1)S(1)}, bf16[1,1,2560,768]{3,2,1,0:T(8,128)(2,1)}, u32[]{:S(2)}) copy-start(bf16[1,1,2560,768]{3,2,1,0:T(8,128)(2,1)} %param.21) | copy-start | bytes 11796484
  159.9 42.8 %all-to-all-start.4 = ((bf16[8,64,2560]{2,1,0:T(8,128)(2,1)}), bf16[8,64,2560]{2,1,0:T(8,128)(2,1)}, u32[]{:S(2)}, u32[]{:S(2)}) async-start(bf16[8,64,2560]{2,1,0:T(8,128)(2,1)} %bitcast.79), calls=%async_computation.4 | async-start | bytes 5242880 | tf_op jit(solution)/shard_map/all_to_all | solution.py:280
  164.3 3.6 %copy-start.27 = (bf16[512,768]{1,0:T(8,128)(2,1)S(1)}, bf16[512,768]{1,0:T(8,128)(2,1)}, u32[]{:S(2)}) copy-start(bf16[512,768]{1,0:T(8,128)(2,1)} %copy-done.26) | copy-start | bytes 2359300
  165.6 36.2 %collective-permute-start = (bf16[128,2560]{1,0:T(8,128)(2,1)S(1)}, bf16[128,2560]{1,0:T(8,128)(2,1)S(1)}, u32[]{:S(2)}, u32[]{:S(2)}) collective-permute-start(bf16[128,2560]{1,0:T(8,128)(2,1)S(1)} %join_forward.1), channel_id=1, source_target_pairs={{0,8},{8,16},{16,24},{24,32},{32,40},{40,48},{48,56},{56,64},{64,7... | collective-permute-start | bytes 1966088 | tf_op jit(solution)/shard_map/ppermute | solution.py:21
  167.9 6.1 %copy-start.29 = (bf16[512,768]{1,0:T(8,128)(2,1)S(1)}, bf16[512,768]{1,0:T(8,128)(2,1)}, u32[]{:S(2)}) copy-start(bf16[512,768]{1,0:T(8,128)(2,1)} %copy-done.28) | copy-start | bytes 2359300
  174.0 6.1 %copy-start.31 = (f32[512,768]{1,0:T(8,128)S(1)}, f32[512,768]{1,0:T(8,128)}, u32[]{:S(2)}) copy-start(f32[512,768]{1,0:T(8,128)} %fusion.10) | copy-start | bytes 4718596
  174.0 6.1 %copy-start.33 = (f32[512,768]{1,0:T(8,128)S(1)}, f32[512,768]{1,0:T(8,128)}, u32[]{:S(2)}) copy-start(f32[512,768]{1,0:T(8,128)} %copy-done.32) | copy-start | bytes 4718596
  180.1 22.6 %copy-start.5 = (bf16[1,128,2560]{2,1,0:T(8,128)(2,1)S(1)}, bf16[1,128,2560]{2,1,0:T(8,128)(2,1)}, u32[]{:S(2)}) copy-start(bf16[1,128,2560]{2,1,0:T(8,128)(2,1)} %param.15) | copy-start | bytes 1966084
  180.1 22.6 %copy-start.9 = (bf16[128,2560]{1,0:T(8,128)(2,1)S(1)}, bf16[128,2560]{1,0:T(8,128)(2,1)}, u32[]{:S(2)}) copy-start(bf16[128,2560]{1,0:T(8,128)(2,1)} %copy-done.8) | copy-start | bytes 1966084
  180.1 22.6 %copy-start.11 = (s32[1,128,2]{2,1,0:T(8,128)S(1)}, s32[1,128,2]{2,1,0:T(8,128)}, u32[]{:S(2)}) copy-start(s32[1,128,2]{2,1,0:T(8,128)} %copy-done.10) | copy-start | bytes 3076
  180.1 22.6 %copy-start.15 = (f32[1,2560]{1,0:T(1,128)S(1)}, f32[1,2560]{1,0:T(1,128)}, u32[]{:S(2)}) copy-start(f32[1,2560]{1,0:T(1,128)} %refs_5_.1) | copy-start | bytes 30724
  180.1 22.6 %copy-start.17 = (f32[128,1]{1,0:T(8,128)S(1)}, f32[128,1]{1,0:T(8,128)}, u32[]{:S(2)}) copy-start(f32[128,1]{1,0:T(8,128)} %copy-done.16) | copy-start | bytes 1540
  205.8 17.0 %collective-permute-start.1 = (bf16[128,2560]{1,0:T(8,128)(2,1)S(1)}, bf16[128,2560]{1,0:T(8,128)(2,1)S(1)}, u32[]{:S(2)}, u32[]{:S(2)}) collective-permute-start(bf16[128,2560]{1,0:T(8,128)(2,1)S(1)} %get-tuple-element.41), channel_id=1, source_target_pairs={{8,0},{16,8},{24,16},{32,24},{40,32},{48,40},{56,48},{64,56},{72,6... | collective-permute-start | bytes 1966088 | tf_op jit(solution)/shard_map/ppermute | solution.py:21
